TPU v7x, 256 devices: a whole 4x4x8 slice. The times are simulated.
256 devices in a mesh: dp: 128 (over z, x_lo, y, core), tensor: 2 (over x_hi).
Axes of the slice: x: 4 (x_hi: 2, x_lo: 2; x = x_hi * 2 + x_lo), y: 4, z: 8, core: 2. Of those that a mesh axis runs over, the one named last changes fastest.
Arguments:
- looked: bfloat16 [8192, 16384], P(('dp', 'tensor')), may hold values from -6 to 6
- column_owner: int32 [8192], replicated, may hold values from 0 to 8191, each once
- v_proj: bfloat16 [384, 8192], P(None, 'tensor'), may hold values from -0.0625 to 0.0625
- u_proj: bfloat16 [384, 8192], P(None, 'tensor'), may hold values from -0.3125 to 0.3125
- bias: float32 [8192], P('tensor'), may hold values from -3 to 3
- upstream: bfloat16 [8192, 16384], P('tensor', 'dp'), may hold values from -6 to 6
Outputs:
- d_looked: bfloat16 [8192, 16384], P(('dp', 'tensor'))
- grad_u: float32 [384, 8192], P('dp', 'tensor')
- grad_v: float32 [384, 8192], P('dp', 'tensor')
- grad_bias: float32 [8192], P('tensor')
Inputs may be any that keep to these rules, and one draw needn't show every extreme that they name: A permutation of the 8192 feature columns: wire row r carries column column_owner[r].
All inputs are finite; a program needn't handle non-finite values.
Results may differ from a plain program's by a relative error of at most 0.0049.
Values may be sent and summed in bfloat16 or wider, within the bound.
No kernel may reach another device: no remote copies, remote signals or barrier semaphores. Data moves between devices by JAX's collectives and lax.ppermute only.
A program may use at most 128 MiB of HBM per device.

v0:
```python
import math

import jax
import jax.numpy as jnp
from jax import lax
from jax.experimental import pallas as pl
from jax.experimental.pallas import tpu as pltpu
from jax.sharding import Mesh, PartitionSpec as P


DP = ("z", "xl", "y", "c")
SWAP = [(0, 1), (1, 0)]
UNROLL = 32
CHUNK = 512


SMEM = pl.BlockSpec(memory_space=pltpu.SMEM)
VMEM = pl.BlockSpec(memory_space=pltpu.VMEM)


def dot_last(left, right, precision=None):
    return lax.dot_general(
        left, right, (((1,), (1,)), ((), ())), precision=precision, preferred_element_type=jnp.float32
    )


def dot_first(left, right):
    return lax.dot_general(
        left, right, (((0,), (0,)), ((), ())), preferred_element_type=jnp.float32
    )


def shift(value, axis, size, by):
    return lax.ppermute(value, axis, [(i, (i + by) % size) for i in range(size)])


def split3(value):
    high = value.astype(jnp.bfloat16)
    rest = value - high.astype(jnp.float32)
    middle = rest.astype(jnp.bfloat16)
    low = (rest - middle.astype(jnp.float32)).astype(jnp.bfloat16)
    return high, middle, low


def join3(parts):
    rows = parts.shape[0] // 4
    wide = parts.astype(jnp.float32)
    return wide[:rows] + wide[rows : 2 * rows] + wide[2 * rows : 3 * rows]


def store3(out, start, value):
    rows = value.shape[0]
    for i, part in enumerate(split3(value)):
        out[start + i * rows : start + (i + 1) * rows, :] = part
    out[start + 3 * rows : start + 4 * rows, :] = jnp.zeros((rows, value.shape[1]), jnp.bfloat16)


def local_call(body, out_shape, *args, scalars=0, mib, specs=None, **kwargs):
    return pl.pallas_call(
        body,
        out_shape=out_shape,
        in_specs=specs or [SMEM] * scalars + [VMEM] * (len(args) - scalars),
        out_specs=jax.tree.map(lambda _: VMEM, out_shape),
        compiler_params=pltpu.CompilerParams(vmem_limit_bytes=mib * 2**20),
        **kwargs,
    )(*args)


def pick_rows(rows, table, picked):
    def step(i, carry):
        for j in range(UNROLL):
            k = i * UNROLL + j
            picked[pl.ds(k, 1), :] = table[pl.ds(rows[k], 1), :]
        return carry

    lax.fori_loop(0, picked.shape[0] // UNROLL, step, 0)


def gather_kernel(rows, near, far, extra, out, table, picked):
    half = near.shape[0]
    dests, height, lanes = out.shape
    block = height - extra.shape[1]
    table[:half] = near[...].astype(jnp.float32)
    table[half:] = far[...].astype(jnp.float32)
    pick_rows(rows, table, picked)
    out[:, :block, :] = picked[...].reshape(dests, block, lanes).astype(out.dtype)
    out[:, block:, :] = extra[...]


def gather(rows, near, far, extra):
    count, lanes = rows.shape[0], near.shape[1]
    dests, height, _ = extra.shape
    return pl.pallas_call(
        gather_kernel,
        out_shape=jax.ShapeDtypeStruct((dests, count // dests + height, lanes), near.dtype),
        in_specs=[SMEM, VMEM, VMEM, VMEM],
        out_specs=VMEM,
        scratch_shapes=[
            pltpu.VMEM((2 * near.shape[0], lanes), jnp.float32),
            pltpu.VMEM((count, lanes), jnp.float32),
        ],
        compiler_params=pltpu.CompilerParams(vmem_limit_bytes=16 * 2**20),
        name="gather_rows",
    )(rows, near, far, extra)


def forward_kernel(rows, near, far, *rest):
    sources, (x_out, part, part16, bias_out, table, picked, *copied, sems) = rest[:3], rest[3:]
    copies = [pltpu.make_async_copy(a, b, sems.at[i]) for i, (a, b) in enumerate(zip(sources, copied))]
    for copy in copies:
        copy.start()
    upstream, v_proj, u_proj = copied
    half, lanes = near.shape
    rank = v_proj.shape[0]
    table[:half] = near[...].astype(jnp.float32)
    table[half:] = far[...].astype(jnp.float32)
    pick_rows(rows, table, picked)
    for copy in copies:
        copy.wait()
    ones = jnp.ones((8, lanes), jnp.float32)
    h_sum = jnp.zeros((rank, lanes), jnp.float32)
    d_sum = jnp.zeros((rank, lanes), jnp.float32)
    for k in range(half // CHUNK):
        here = slice(k * CHUNK, (k + 1) * CHUNK)
        x = picked[here, :]
        scaled = upstream[here, :].astype(jnp.float32) * x
        x16 = x.astype(jnp.bfloat16)
        x_out[here, :] = x16
        sums = dot_last(ones, scaled, lax.Precision.HIGHEST)
        for j in range(CHUNK // 128):
            row = k * (CHUNK // 128) + j
            bias_out[row : row + 1, :] = sums[:1, j * 128 : (j + 1) * 128]
        h_sum += jnp.dot(v_proj[:, here], x16, preferred_element_type=jnp.float32)
        d_sum += jnp.dot(
            u_proj[:, here], scaled.astype(jnp.bfloat16), preferred_element_type=jnp.float32
        )
    part[:rank] = h_sum
    part[rank:] = d_sum
    part16[:rank] = h_sum.astype(jnp.bfloat16)
    part16[rank:] = d_sum.astype(jnp.bfloat16)


def ranks_kernel(part, other, bias, ranks, message, total):
    rows = part.shape[0]
    value = part[...] + other[...].astype(jnp.float32)
    ranks[...] = value.astype(jnp.bfloat16)
    total[...] = value
    step = rows // 2 // 128
    for i in range(2):
        for j in range(step):
            to = i * rows // 2 + j * 128
            rank_rows = total[pl.ds(i * rows // 2 + j, 128, stride=step), :]
            message[to : to + 128, :] = rank_rows.astype(jnp.bfloat16)
    store3(message, rows, bias[...])


def join_kernel(*rest):
    *blocks, message = rest
    rows = (message.shape[0] - 128) // len(blocks)
    bias = jnp.zeros((32, 128), jnp.float32)
    for k, block in enumerate(blocks):
        message[k * rows : (k + 1) * rows, :] = block[:rows, :]
        bias += join3(block[rows:, :])
    store3(message, len(blocks) * rows, bias)


def join_blocks(blocks):
    rows, lanes = blocks[0].shape
    shape = jax.ShapeDtypeStruct(((rows - 128) * len(blocks) + 128, lanes), blocks[0].dtype)
    return local_call(join_kernel, shape, *blocks, mib=6)


def grads_kernel(place, x_group, up_group, near_ranks, far_ranks, pieces, result, spread, bias_rows):
    count, wide, lanes = x_group.shape
    ny = count // 2
    y, c = place[0], place[1]
    both = near_ranks.shape[0] // ny // 128 * 128
    rank = both // 2
    for part in range(2):
        acc = jnp.zeros((rank, wide), jnp.float32)
        for k in range(ny):
            here = slice(k * both + part * rank, k * both + (part + 1) * rank)
            pair = lax.rem(y + ny - k, ny) * 2
            left = jnp.concatenate([near_ranks[here, :], far_ranks[here, :]], axis=1)
            right = [x_group[pair + c], x_group[pair + 1 - c]]
            if part == 0:
                ups = [up_group[pair + c], up_group[pair + 1 - c]]
                right = [
                    (up.astype(jnp.float32) * x.astype(jnp.float32)).astype(jnp.bfloat16)
                    for up, x in zip(ups, right)
                ]
            acc = acc + dot_last(left, jnp.concatenate(right, axis=1))
        result[:, part * wide : (part + 1) * wide] = acc
    dests, height, _ = pieces.shape
    blocks = 2 * wide // lanes
    for j in range(rank // dests):
        for k in range(blocks):
            spread[pl.ds(j * blocks + k, dests, stride=height), :] = result[
                j * dests : (j + 1) * dests, k * lanes : (k + 1) * lanes
            ]
    bias = join3(near_ranks[ny * both :, :]) + join3(far_ranks[ny * both :, :])
    bias_rows[...] = bias
    mine = (y * 2 + c) * (wide // lanes)
    first = rank // dests * blocks
    for k in range(wide // lanes):
        row = bias_rows[pl.ds(mine + k, 1), :]
        high = row.astype(jnp.bfloat16).astype(jnp.float32)
        for i, value in enumerate((high, row - high)):
            at = first + i * (wide // lanes) + k
            spread[pl.ds(at, dests, stride=height), :] = jnp.broadcast_to(value, (dests, lanes))
    pieces[...] = spread[...].reshape(dests, height, lanes).astype(jnp.bfloat16)


def arrive_kernel(got, d_looked, grad_u, grad_v, grad_bias, *, block, wide, norm):
    sources, height, lanes = got.shape
    for k in range(sources):
        d_looked[:, k * lanes : (k + 1) * lanes] = got[k, :block, :]
    columns = wide // lanes
    group = grad_u.shape[1] // wide
    first = 2 * columns * grad_u.shape[0]
    for b in range(group):
        total = jnp.zeros((height - block, lanes), jnp.float32)
        for k in range(sources // group):
            total += got[k * group + b, block:, :].astype(jnp.float32)
        total = total * norm
        for k in range(columns):
            here = slice(b * wide + k * lanes, b * wide + (k + 1) * lanes)
            for j in range(grad_u.shape[0]):
                row = j * 2 * columns + k
                grad_u[j : j + 1, here] = total[row : row + 1]
                grad_v[j : j + 1, here] = total[row + columns : row + columns + 1]
            row = first + k
            grad_bias[b * columns + k : b * columns + k + 1, :] = (
                total[row : row + 1] + total[row + columns : row + columns + 1]
            )


def inverse_rows(column_owner, first_column, count):
    wires = jnp.arange(column_owner.shape[0], dtype=jnp.int32)
    high = column_owner // 128 - first_column // 128
    low = column_owner % 128
    pick = (high[None, :] == jnp.arange(count // 128, dtype=jnp.int32)[:, None]).astype(jnp.bfloat16)
    lanes = low[:, None] == jnp.arange(128, dtype=jnp.int32)[None, :]
    values = jnp.concatenate(
        [
            jnp.where(lanes, (wires // 128)[:, None].astype(jnp.bfloat16), 0),
            jnp.where(lanes, (wires % 128)[:, None].astype(jnp.bfloat16), 0),
        ],
        axis=1,
    )
    found = jnp.dot(pick, values, preferred_element_type=jnp.float32).astype(jnp.int32)
    return (found[:, :128] * 128 + found[:, 128:]).reshape(-1)


def step(looked, column_owner, v_proj, u_proj, bias, upstream):
    y, c, t = (lax.axis_index(a).astype(jnp.int32) for a in ("y", "c", "t"))
    ny = lax.axis_size("y")
    dp_count = lax.axis_size(DP)
    block_rows = looked.shape[0]
    rank, half_width = v_proj.shape
    samples = upstream.shape[1]
    norm = 1.0 / math.sqrt(samples * dp_count)
    bf16 = jnp.bfloat16

    array = jax.ShapeDtypeStruct
    group = 2 * ny
    wide = half_width // group
    arrived = lax.all_to_all(looked, DP, split_axis=1, concat_axis=0, tiled=True)
    partner = lax.ppermute(arrived, "t", SWAP)
    up_group = lax.all_to_all(
        upstream.reshape(group, wide, samples), ("y", "c"), split_axis=0, concat_axis=0, tiled=True
    )
    wire = inverse_rows(column_owner, t * half_width, half_width)
    side = wire // block_rows % 2
    spot = wire // (2 * block_rows) * block_rows + wire % block_rows
    x_rows = jnp.where(side == t, 0, half_width) + spot
    hbm = pltpu.with_memory_space_constraint
    x_zero, part, part16, bias_part = local_call(
        forward_kernel,
        [
            array((half_width, samples), bf16),
            array((2 * rank, samples), jnp.float32),
            array((2 * rank, samples), bf16),
            array((half_width // 128, 128), jnp.float32),
        ],
        x_rows,
        arrived,
        partner,
        upstream,
        hbm(v_proj, pltpu.HBM),
        hbm(u_proj, pltpu.HBM),
        scalars=1,
        scratch_shapes=[
            pltpu.VMEM((2 * half_width, samples), jnp.float32),
            pltpu.VMEM((half_width, samples), jnp.float32),
            pltpu.VMEM(upstream.shape, bf16),
            pltpu.VMEM(v_proj.shape, bf16),
            pltpu.VMEM(u_proj.shape, bf16),
            pltpu.SemaphoreType.DMA((3,)),
        ],
        specs=[SMEM, VMEM, VMEM] + [pl.BlockSpec(memory_space=pltpu.HBM)] * 3,
        mib=28,
    )
    other = lax.ppermute(part16, "t", SWAP)
    x_group = lax.all_to_all(
        x_zero.reshape(group, wide, samples), ("y", "c"), split_axis=0, concat_axis=0, tiled=True
    )
    ranks, message = local_call(
        ranks_kernel,
        [array((2 * rank, samples), bf16), array((2 * rank + 128, samples), bf16)],
        part,
        other,
        bias_part,
        scratch_shapes=[pltpu.VMEM((2 * rank, samples), jnp.float32)],
        mib=4,
    )

    mix = dot_first(u_proj, ranks[:rank]) + bias[:, None]
    cotan = upstream.astype(jnp.float32)
    dx_zero = (cotan * (mix + 1.0) + dot_first(v_proj, ranks[rank:])).astype(bf16)
    dx_other = lax.ppermute(dx_zero, "t", SWAP)

    blocks = [message]
    for k in range(1, ny):
        blocks.append(shift(blocks[0], "y", ny, k))
    near_ranks = join_blocks(blocks)
    far_ranks = lax.ppermute(near_ranks, "c", SWAP)
    height = rank // dp_count * (2 * wide // 128) + 2 * wide // 128
    pieces = local_call(
        grads_kernel,
        array((dp_count, height, 128), bf16),
        jnp.stack([y, c]),
        x_group,
        up_group,
        near_ranks,
        far_ranks,
        scalars=1,
        scratch_shapes=[
            pltpu.VMEM((rank, 2 * wide), jnp.float32),
            pltpu.VMEM((dp_count * height, 128), jnp.float32),
            pltpu.VMEM((32, 128), jnp.float32),
        ],
        mib=16,
    )

    columns = lax.dynamic_index_in_dim(
        column_owner.reshape(dp_count, 2, block_rows), t, 1, keepdims=False
    ).reshape(-1)
    out_rows = jnp.where(columns // half_width == t, 0, half_width) + columns % half_width
    outgoing = gather(out_rows, dx_zero, dx_other, pieces)
    got = lax.all_to_all(outgoing, DP, split_axis=0, concat_axis=0, tiled=True)
    d_looked, grad_u, grad_v, grad_bias = local_call(
        lambda *refs: arrive_kernel(*refs, block=block_rows, wide=wide, norm=norm),
        [
            array((block_rows, dp_count * samples), bf16),
            array((rank // dp_count, half_width), jnp.float32),
            array((rank // dp_count, half_width), jnp.float32),
            array((half_width // 128, 128), jnp.float32),
        ],
        got,
        mib=8,
    )
    return (d_looked, grad_u, grad_v, grad_bias.reshape(-1))


def solution(mesh):
    fine = Mesh(mesh.devices.reshape(8, 2, 4, 2, 2), DP + ("t",))
    in_specs = (
        P(DP + ("t",), None),
        P(),
        P(None, "t"),
        P(None, "t"),
        P("t"),
        P("t", DP),
    )
    out_specs = (P(DP + ("t",), None), P(DP, "t"), P(DP, "t"), P("t"))
    return jax.shard_map(step, mesh=fine, in_specs=in_specs, out_specs=out_specs, check_vma=False)
```

profile of v0, /device:TPU:4, one launch (start us, length us, event | category | flops | bytes accessed | tf_op | source)
XLA Modules:
  0.0 192.1 jit_solution(17818445487594519763)
XLA Ops:
  0.7 1.2 copy-done
  1.9 1.1 copy_bitcast_fusion
  3.0 14.0 %all-to-all-start = ((bf16[32,128,128]{2,0,1:T(8,128)(2,1)}), bf16[32,128,128]{2,0,1:T(8,128)(2,1)S(1)}, u32[]{:S(2)}, u32[]{:S(2)}) async-start(bf16[32,128,128]{2,0,1:T(8,128)(2,1)} %copy_bitcast_fusion), calls=%async_computation | async-start | bytes 2097152 | tf_op jit(solution)/shard_map/all_to_all | solution.py:268
  17.1 29.2 %all-to-all-done = bf16[32,128,128]{2,0,1:T(8,128)(2,1)S(1)} async-done(((bf16[32,128,128]{2,0,1:T(8,128)(2,1)}), bf16[32,128,128]{2,0,1:T(8,128)(2,1)S(1)}, u32[]{:S(2)}, u32[]{:S(2)}) %all-to-all-start) | async-done | bytes 1048608 | tf_op jit(solution)/shard_map/all_to_all | solution.py:268
  47.1 3.8 %fusion.10 = (bf16[8192,128]{1,0:T(8,128)(2,1)S(1)}, bf16[8192,128]{1,0:T(8,128)(2,1)S(1)}) fusion(s32[8192]{0:T(1024)S(1)} %get-tuple-element.25, bf16[8192]{0:T(1024)(128)(2,1)S(1)} %get-tuple-element.28, bf16[8192]{0:T(1024)(128)(2,1)S(1)} %fusion.25), kind=kLoop, calls=%fused_computation.13 | loop fusion | flops 3145728 | bytes 4259840 | tf_op jit(solution)/shard_map/jit(_where)/select_n | solution.py:246
  51.7 20.2 %collective-permute-done.far = bf16[4096,128]{1,0:T(8,128)(2,1)S(1)} collective-permute-done((bf16[4096,128]{1,0:T(8,128)(2,1)S(1)}, bf16[4096,128]{1,0:T(8,128)(2,1)S(1)}, u32[]{:S(2)}, u32[]{:S(2)}) %collective-permute-start) | collective-permute-done | bytes 1048608 | tf_op jit(solution)/shard_map/ppermute | solution.py:269
  72.0 8.5 %shard_map.93 = (bf16[4096,128]{1,0:T(8,128)(2,1)S(1)}, f32[768,128]{1,0:T(8,128)S(1)}, bf16[768,128]{1,0:T(8,128)(2,1)S(1)}, f32[32,128]{1,0:T(8,128)S(1)}) custom-call(s32[4096]{0:T(1024)S(1)} %fusion.36.rows, bf16[4096,128]{1,0:T(8,128)(2,1)S(1)} %bitcast.30, bf16[4096,128]{1,0:T(8,128)(2,1)S(1)} %collective-permute-done.far, bf16[4096,128]{1,0:T(8,128)(2,1)} %rest_0_.1, ...), custom_call_target="tpu_custom_call" | custom-call | tf_op jit(solution)/shard_map/pallas_call | solution.py:59
  80.4 1.0 copy-done.1
  82.2 3.8 %all-to-all-start.2 = ((bf16[8,512,128]{2,1,0:T(8,128)(2,1)}), bf16[8,512,128]{2,1,0:T(8,128)(2,1)S(1)}, u32[]{:S(2)}, u32[]{:S(2)}) async-start(bf16[8,512,128]{2,1,0:T(8,128)(2,1)} %bitcast.9), calls=%async_computation.2 | async-start | bytes 2097152 | tf_op jit(solution)/shard_map/all_to_all | solution.py:270
  86.0 2.6 %collective-permute-done.1.other = bf16[768,128]{1,0:T(8,128)(2,1)S(1)} collective-permute-done((bf16[768,128]{1,0:T(8,128)(2,1)S(1)}, bf16[768,128]{1,0:T(8,128)(2,1)S(1)}, u32[]{:S(2)}, u32[]{:S(2)}) %collective-permute-start.1) | collective-permute-done | bytes 196640 | tf_op jit(solution)/shard_map/ppermute | solution.py:304
  88.7 1.1 collective-permute-start.3
  89.7 3.3 %collective-permute-start.4 = (bf16[896,128]{1,0:T(8,128)(2,1)S(1)}, bf16[896,128]{1,0:T(8,128)(2,1)}, u32[]{:S(2)}, u32[]{:S(2)}) collective-permute-start(bf16[896,128]{1,0:T(8,128)(2,1)S(1)} %get-tuple-element.19.rest_0_), channel_id=1, source_target_pairs={{0,8},{4,12},{8,0},{12,4},{1,9},{5,13},{9,1},{13,5},{2,10},{6,14},... | collective-permute-start | bytes 688136 | tf_op jit(solution)/shard_map/ppermute | solution.py:34
  93.6 3.8 %fusion.3 = f32[4096,128]{1,0:T(8,128)S(1)} fusion(bf16[384,4096]{1,0:T(8,128)(2,1)} %rest_2_.1, bf16[4096,128]{1,0:T(8,128)(2,1)} %rest_0_.1, f32[4096]{0:T(1024)S(1)} %copy-done.4, bf16[768,128]{1,0:T(8,128)(2,1)S(1)} %get-tuple-element.17), kind=kOutput, calls=%fused_computation.5 | convolution fusion | flops 404750336 | bytes 6406144 | tf_op jit(solution)/shard_map/dot_general | solution.py:28
  97.4 1.5 fusion.4.near
  98.9 1.6 collective-permute-start.2
  100.4 2.1 %all-to-all-done.2.up_group = bf16[8,512,128]{2,1,0:T(8,128)(2,1)S(1)} async-done(((bf16[8,512,128]{2,1,0:T(8,128)(2,1)}), bf16[8,512,128]{2,1,0:T(8,128)(2,1)S(1)}, u32[]{:S(2)}, u32[]{:S(2)}) %all-to-all-start.2) | async-done | bytes 1048608 | tf_op jit(solution)/shard_map/all_to_all | solution.py:270
  102.5 4.2 %all-to-all-start.1 = ((bf16[8,512,128]{2,1,0:T(8,128)(2,1)}), bf16[8,512,128]{2,1,0:T(8,128)(2,1)}, u32[]{:S(2)}, u32[]{:S(2)}) async-start(bf16[8,512,128]{2,1,0:T(8,128)(2,1)} %bitcast.31), calls=%async_computation.1 | async-start | bytes 2097152 | tf_op jit(solution)/shard_map/all_to_all | solution.py:305
  106.9 5.5 %collective-permute-done.4.rest_2_ = bf16[896,128]{1,0:T(8,128)(2,1)} collective-permute-done((bf16[896,128]{1,0:T(8,128)(2,1)S(1)}, bf16[896,128]{1,0:T(8,128)(2,1)}, u32[]{:S(2)}, u32[]{:S(2)}) %collective-permute-start.4) | collective-permute-done | bytes 229408 | tf_op jit(solution)/shard_map/ppermute | solution.py:34
  112.4 2.1 %shard_map.95.near_ranks = bf16[3200,128]{1,0:T(8,128)(2,1)} custom-call(bf16[896,128]{1,0:T(8,128)(2,1)S(1)} %get-tuple-element.19.rest_0_, bf16[896,128]{1,0:T(8,128)(2,1)} %collective-permute-done.3.rest_1_, bf16[896,128]{1,0:T(8,128)(2,1)} %collective-permute-done.4.rest_2_, bf16[896,128]{1,0:T(8,128)(2,1)} %collective-permute-done.5.rest_3_), custom_call_target="tpu_custom_call" | custom-call | tf_op jit(solution)/shard_map/pallas_call | solution.py:59
  115.1 8.0 %all-to-all-done.1.x_group = bf16[8,512,128]{2,1,0:T(8,128)(2,1)} async-done(((bf16[8,512,128]{2,1,0:T(8,128)(2,1)}), bf16[8,512,128]{2,1,0:T(8,128)(2,1)}, u32[]{:S(2)}, u32[]{:S(2)}) %all-to-all-start.1) | async-done | bytes 1048608 | tf_op jit(solution)/shard_map/all_to_all | solution.py:305
  123.1 4.1 %shard_map.96.extra = bf16[128,32,128]{2,1,0:T(8,128)(2,1)S(1)} custom-call(s32[2]{0:T(128)S(1)} %pad_add_fusion.place, bf16[8,512,128]{2,1,0:T(8,128)(2,1)} %all-to-all-done.1.x_group, bf16[8,512,128]{2,1,0:T(8,128)(2,1)S(1)} %all-to-all-done.2.up_group, bf16[3200,128]{1,0:T(8,128)(2,1)} %shard_map.95.near_ranks, ...), custom_call_target="tpu_custom_call" | custom-call | tf_op jit(solution)/shard_map/pallas_call | solution.py:59
  127.2 5.5 %gather_rows.1 = bf16[128,64,128]{2,1,0:T(8,128)(2,1)S(1)} custom-call(s32[4096]{0:T(1024)S(1)} %fusion.30.rows, bf16[4096,128]{1,0:T(8,128)(2,1)S(1)} %fusion.4.near, bf16[4096,128]{1,0:T(8,128)(2,1)} %collective-permute-done.2.far, bf16[128,32,128]{2,1,0:T(8,128)(2,1)S(1)} %shard_map.96.extra), custom_call_target="tpu_custom_call" | custom-call | tf_op jit(solution)/shard_map/gather_rows/pallas_call | solution.py:93
  132.7 58.1 %all_to_all.34.refs_0_ = bf16[128,64,128]{2,1,0:T(8,128)(2,1)S(1)} all-to-all(bf16[128,64,128]{2,1,0:T(8,128)(2,1)S(1)} %gather_rows.1), channel_id=1, replica_groups=mesh['z'=8,'xl'=2,'y'=4,'c'=2,'t'=2] {'z','xl','y','c'}, dimensions={0} | all-to-all | bytes 4194304 | tf_op jit(solution)/shard_map/all_to_all | solution.py:351
  190.8 1.3 shard_map.97
  (26 shorter events, 3.7 us)
Async XLA Ops:
  0.6 1.2 copy-start
  0.6 16.4 %copy-start.3 = (s32[8192]{0:T(1024)S(1)}, s32[8192]{0:T(1024)}, u32[]{:S(2)}) copy-start(s32[8192]{0:T(1024)} %param.7) | copy-start | bytes 98308
  3.0 43.2 %all-to-all-start = ((bf16[32,128,128]{2,0,1:T(8,128)(2,1)}), bf16[32,128,128]{2,0,1:T(8,128)(2,1)S(1)}, u32[]{:S(2)}, u32[]{:S(2)}) async-start(bf16[32,128,128]{2,0,1:T(8,128)(2,1)} %copy_bitcast_fusion), calls=%async_computation | async-start | bytes 2097152 | tf_op jit(solution)/shard_map/all_to_all | solution.py:268
  46.3 25.7 %collective-permute-start = (bf16[4096,128]{1,0:T(8,128)(2,1)S(1)}, bf16[4096,128]{1,0:T(8,128)(2,1)S(1)}, u32[]{:S(2)}, u32[]{:S(2)}) collective-permute-start(bf16[4096,128]{1,0:T(8,128)(2,1)S(1)} %bitcast.29), channel_id=1, source_target_pairs={{0,1},{1,0},{2,3},{3,2},{4,5},{5,4},{6,7},{7,6},{8,9},{9,8},{10,11... | collective-permute-start | bytes 3145736 | tf_op jit(solution)/shard_map/ppermute | solution.py:269
  80.4 1.0 copy-start.1
  81.4 12.2 %copy-start.4 = (f32[4096]{0:T(1024)S(1)}, f32[4096]{0:T(1024)}, u32[]{:S(2)}) copy-start(f32[4096]{0:T(1024)} %param.10) | copy-start | bytes 49156
  81.4 7.2 %collective-permute-start.1 = (bf16[768,128]{1,0:T(8,128)(2,1)S(1)}, bf16[768,128]{1,0:T(8,128)(2,1)S(1)}, u32[]{:S(2)}, u32[]{:S(2)}) collective-permute-start(bf16[768,128]{1,0:T(8,128)(2,1)S(1)} %get-tuple-element.15), channel_id=1, source_target_pairs={{0,1},{1,0},{2,3},{3,2},{4,5},{5,4},{6,7},{7,6},{8,9},{9,8},{10,11... | collective-permute-start | bytes 589832 | tf_op jit(solution)/shard_map/ppermute | solution.py:304
  82.2 20.3 %all-to-all-start.2 = ((bf16[8,512,128]{2,1,0:T(8,128)(2,1)}), bf16[8,512,128]{2,1,0:T(8,128)(2,1)S(1)}, u32[]{:S(2)}, u32[]{:S(2)}) async-start(bf16[8,512,128]{2,1,0:T(8,128)(2,1)} %bitcast.9), calls=%async_computation.2 | async-start | bytes 2097152 | tf_op jit(solution)/shard_map/all_to_all | solution.py:270
  88.7 18.2 %collective-permute-start.3 = (bf16[896,128]{1,0:T(8,128)(2,1)S(1)}, bf16[896,128]{1,0:T(8,128)(2,1)}, u32[]{:S(2)}, u32[]{:S(2)}) collective-permute-start(bf16[896,128]{1,0:T(8,128)(2,1)S(1)} %get-tuple-element.19.rest_0_), channel_id=1, source_target_pairs={{0,4},{4,8},{8,12},{12,0},{1,5},{5,9},{9,13},{13,1},{2,6},{6,10},{... | collective-permute-start | bytes 688136 | tf_op jit(solution)/shard_map/ppermute | solution.py:34
  89.7 22.7 %collective-permute-start.4 = (bf16[896,128]{1,0:T(8,128)(2,1)S(1)}, bf16[896,128]{1,0:T(8,128)(2,1)}, u32[]{:S(2)}, u32[]{:S(2)}) collective-permute-start(bf16[896,128]{1,0:T(8,128)(2,1)S(1)} %get-tuple-element.19.rest_0_), channel_id=1, source_target_pairs={{0,8},{4,12},{8,0},{12,4},{1,9},{5,13},{9,1},{13,5},{2,10},{6,14},... | collective-permute-start | bytes 688136 | tf_op jit(solution)/shard_map/ppermute | solution.py:34
  93.1 19.3 %collective-permute-start.5 = (bf16[896,128]{1,0:T(8,128)(2,1)S(1)}, bf16[896,128]{1,0:T(8,128)(2,1)}, u32[]{:S(2)}, u32[]{:S(2)}) collective-permute-start(bf16[896,128]{1,0:T(8,128)(2,1)S(1)} %get-tuple-element.19.rest_0_), channel_id=1, source_target_pairs={{0,12},{4,0},{8,4},{12,8},{1,13},{5,1},{9,5},{13,9},{2,14},{6,2},{... | collective-permute-start | bytes 688136 | tf_op jit(solution)/shard_map/ppermute | solution.py:34
  93.6 3.8 %copy-start.2 = (bf16[384,4096]{1,0:T(8,128)(2,1)S(1)}, bf16[384,4096]{1,0:T(8,128)(2,1)}, u32[]{:S(2)}) copy-start(bf16[384,4096]{1,0:T(8,128)(2,1)} %rest_1_.1) | copy-start | bytes 9437188
  98.9 28.3 %collective-permute-start.2 = (bf16[4096,128]{1,0:T(8,128)(2,1)S(1)}, bf16[4096,128]{1,0:T(8,128)(2,1)}, u32[]{:S(2)}, u32[]{:S(2)}) collective-permute-start(bf16[4096,128]{1,0:T(8,128)(2,1)S(1)} %fusion.4.near), channel_id=1, source_target_pairs={{0,1},{1,0},{2,3},{3,2},{4,5},{5,4},{6,7},{7,6},{8,9},{9,8},{10,11... | collective-permute-start | bytes 3145736 | tf_op jit(solution)/shard_map/ppermute | solution.py:321
  102.5 20.6 %all-to-all-start.1 = ((bf16[8,512,128]{2,1,0:T(8,128)(2,1)}), bf16[8,512,128]{2,1,0:T(8,128)(2,1)}, u32[]{:S(2)}, u32[]{:S(2)}) async-start(bf16[8,512,128]{2,1,0:T(8,128)(2,1)} %bitcast.31), calls=%async_computation.1 | async-start | bytes 2097152 | tf_op jit(solution)/shard_map/all_to_all | solution.py:305
  114.5 8.6 %collective-permute-start.6 = (bf16[3200,128]{1,0:T(8,128)(2,1)}, bf16[3200,128]{1,0:T(8,128)(2,1)}, u32[]{:S(2)}, u32[]{:S(2)}) collective-permute-start(bf16[3200,128]{1,0:T(8,128)(2,1)} %shard_map.95.near_ranks), channel_id=1, source_target_pairs={{0,2},{2,0},{1,3},{3,1},{4,6},{6,4},{5,7},{7,5},{8,10},{10,8},{9,1... | collective-permute-start | bytes 2457608 | tf_op jit(solution)/shard_map/ppermute | solution.py:327
where the time goes:
time: 195 us; the launch traced here: 192 us
  waiting for transfers between devices  67.7 us (35%)
  blocking collectives  58.1 us (30%)
  starting transfers between devices  30 us (15%)
  Pallas kernels  21.5 us (11%)
  matrix products  6.09 us (3%)
  other arithmetic  3.99 us (2%)
  local copies, waits for them, and re-layouts  3.77 us (2%)
    all_to_all x1, blocking collectives, step(): got = lax.all_to_all(outgoing, DP, split_axis=0, concat_axis=0, tiled=True)  58.1 us
    all_to_all x1, waiting for transfers between devices, step(): lax.all_to_all(looked, DP, split_axis=1, concat_axis=0, tiled=True)  29.2 us
    ppermute x1, waiting for transfers between devices, step(): partner = lax.ppermute(arrived, 't', SWAP)  20.2 us
    pallas_call x5, Pallas kernels, local_call(): pl.pallas_call(body, out_shape=out_shape, in_specs=specs or [SMEM] * scal...  16 us
    all_to_all x1, starting transfers between devices, step(): lax.all_to_all(looked, DP, split_axis=1, concat_axis=0, tiled=True)  14 us
    all_to_all x1, waiting for transfers between devices, step(): lax.all_to_all(x_zero.reshape(group, wide, samples), ('y', 'c'), split_ax...  8.03 us
    ppermute x3, waiting for transfers between devices, shift(): lax.ppermute(value, axis, [(i, (i + by) % size) for i in range(size)])  5.62 us
    pallas_call x1, Pallas kernels, gather(): pl.pallas_call(gather_kernel, out_shape=jax.ShapeDtypeStruct((dests, coun...  5.46 us
  transfers between devices with their start and end apart: 10, of which 7 were waited for; matrix products, arithmetic and copies ran while one was open for 5% of the time, Pallas kernels for 3%

commit v1 on v0

--- a/solution.py
+++ b/solution.py
@@ -18,15 +18,9 @@
 VMEM = pl.BlockSpec(memory_space=pltpu.VMEM)
 
 
-def dot_last(left, right, precision=None):
+def dot_last(left, right):
     return lax.dot_general(
-        left, right, (((1,), (1,)), ((), ())), precision=precision, preferred_element_type=jnp.float32
-    )
-
-
-def dot_first(left, right):
-    return lax.dot_general(
-        left, right, (((0,), (0,)), ((), ())), preferred_element_type=jnp.float32
+        left, right, (((1,), (1,)), ((), ())), preferred_element_type=jnp.float32
     )
 
 
@@ -105,7 +99,7 @@
 
 
 def forward_kernel(rows, near, far, *rest):
-    sources, (x_out, part, part16, bias_out, table, picked, *copied, sems) = rest[:3], rest[3:]
+    sources, (x_out, part, part16, table, picked, *copied, sems) = rest[:3], rest[3:]
     copies = [pltpu.make_async_copy(a, b, sems.at[i]) for i, (a, b) in enumerate(zip(sources, copied))]
     for copy in copies:
         copy.start()
@@ -117,7 +111,7 @@
     pick_rows(rows, table, picked)
     for copy in copies:
         copy.wait()
-    ones = jnp.ones((8, lanes), jnp.float32)
+    ones = jnp.ones((8, 3 * lanes), jnp.bfloat16)
     h_sum = jnp.zeros((rank, lanes), jnp.float32)
     d_sum = jnp.zeros((rank, lanes), jnp.float32)
     for k in range(half // CHUNK):
@@ -126,62 +120,68 @@
         scaled = upstream[here, :].astype(jnp.float32) * x
         x16 = x.astype(jnp.bfloat16)
         x_out[here, :] = x16
-        sums = dot_last(ones, scaled, lax.Precision.HIGHEST)
+        sums = dot_last(ones, jnp.concatenate(split3(scaled), axis=1))
         for j in range(CHUNK // 128):
             row = k * (CHUNK // 128) + j
-            bias_out[row : row + 1, :] = sums[:1, j * 128 : (j + 1) * 128]
+            part[2 * rank + row : 2 * rank + row + 1, :] = sums[:1, j * 128 : (j + 1) * 128]
         h_sum += jnp.dot(v_proj[:, here], x16, preferred_element_type=jnp.float32)
         d_sum += jnp.dot(
             u_proj[:, here], scaled.astype(jnp.bfloat16), preferred_element_type=jnp.float32
         )
     part[:rank] = h_sum
-    part[rank:] = d_sum
+    part[rank : 2 * rank] = d_sum
     part16[:rank] = h_sum.astype(jnp.bfloat16)
     part16[rank:] = d_sum.astype(jnp.bfloat16)
 
 
-def ranks_kernel(part, other, bias, ranks, message, total):
-    rows = part.shape[0]
-    value = part[...] + other[...].astype(jnp.float32)
-    ranks[...] = value.astype(jnp.bfloat16)
+def ranks_kernel(part, other, bias, upstream_in, v_in, u_in, message, dx, upstream, v_proj, u_proj, total, sems):
+    rows = other.shape[0]
+    rank = rows // 2
+    count = upstream.shape[0] // CHUNK
+    copies = []
+    for k in range(count):
+        here = slice(k * CHUNK, (k + 1) * CHUNK)
+        pairs = (
+            (u_in.at[:, here], u_proj.at[:, here]),
+            (v_in.at[:, here], v_proj.at[:, here]),
+            (upstream_in.at[here], upstream.at[here]),
+        )
+        copies.append([pltpu.make_async_copy(a, b, sems.at[k, i]) for i, (a, b) in enumerate(pairs)])
+        for copy in copies[-1]:
+            copy.start()
+    value = part[:rows] + other[...].astype(jnp.float32)
     total[...] = value
-    step = rows // 2 // 128
+    step = rank // 128
     for i in range(2):
         for j in range(step):
-            to = i * rows // 2 + j * 128
-            rank_rows = total[pl.ds(i * rows // 2 + j, 128, stride=step), :]
+            to = i * rank + j * 128
+            rank_rows = total[pl.ds(i * rank + j, 128, stride=step), :]
             message[to : to + 128, :] = rank_rows.astype(jnp.bfloat16)
-    store3(message, rows, bias[...])
-
-
-def join_kernel(*rest):
-    *blocks, message = rest
-    rows = (message.shape[0] - 128) // len(blocks)
-    bias = jnp.zeros((32, 128), jnp.float32)
-    for k, block in enumerate(blocks):
-        message[k * rows : (k + 1) * rows, :] = block[:rows, :]
-        bias += join3(block[rows:, :])
-    store3(message, len(blocks) * rows, bias)
-
-
-def join_blocks(blocks):
-    rows, lanes = blocks[0].shape
-    shape = jax.ShapeDtypeStruct(((rows - 128) * len(blocks) + 128, lanes), blocks[0].dtype)
-    return local_call(join_kernel, shape, *blocks, mib=6)
-
-
-def grads_kernel(place, x_group, up_group, near_ranks, far_ranks, pieces, result, spread, bias_rows):
+    store3(message, rows, part[rows:])
+    h_turned = value[:rank].T.astype(jnp.bfloat16)
+    d_turned = value[rank:].T.astype(jnp.bfloat16)
+    for k in range(count):
+        here = slice(k * CHUNK, (k + 1) * CHUNK)
+        for copy in copies[k]:
+            copy.wait()
+        mix = jnp.dot(h_turned, u_proj[:, here], preferred_element_type=jnp.float32)
+        mix = (mix + bias[k : k + 1, :]).T
+        back = jnp.dot(d_turned, v_proj[:, here], preferred_element_type=jnp.float32).T
+        dx[here, :] = (upstream[here, :].astype(jnp.float32) * (mix + 1.0) + back).astype(jnp.bfloat16)
+
+
+def grads_kernel(place, x_group, up_group, *rest):
+    *ranks, pieces, result, spread, bias_rows = rest
     count, wide, lanes = x_group.shape
     ny = count // 2
     y, c = place[0], place[1]
-    both = near_ranks.shape[0] // ny // 128 * 128
-    rank = both // 2
+    rank = (ranks[0].shape[0] - 128) // 2
     for part in range(2):
+        here = slice(part * rank, (part + 1) * rank)
         acc = jnp.zeros((rank, wide), jnp.float32)
         for k in range(ny):
-            here = slice(k * both + part * rank, k * both + (part + 1) * rank)
             pair = lax.rem(y + ny - k, ny) * 2
-            left = jnp.concatenate([near_ranks[here, :], far_ranks[here, :]], axis=1)
+            left = jnp.concatenate([ranks[k][here, :], ranks[ny + k][here, :]], axis=1)
             right = [x_group[pair + c], x_group[pair + 1 - c]]
             if part == 0:
                 ups = [up_group[pair + c], up_group[pair + 1 - c]]
@@ -198,8 +198,7 @@
             spread[pl.ds(j * blocks + k, dests, stride=height), :] = result[
                 j * dests : (j + 1) * dests, k * lanes : (k + 1) * lanes
             ]
-    bias = join3(near_ranks[ny * both :, :]) + join3(far_ranks[ny * both :, :])
-    bias_rows[...] = bias
+    bias_rows[...] = sum(join3(block[2 * rank :, :]) for block in ranks)
     mine = (y * 2 + c) * (wide // lanes)
     first = rank // dests * blocks
     for k in range(wide // lanes):
@@ -275,18 +274,17 @@
     spot = wire // (2 * block_rows) * block_rows + wire % block_rows
     x_rows = jnp.where(side == t, 0, half_width) + spot
     hbm = pltpu.with_memory_space_constraint
-    x_zero, part, part16, bias_part = local_call(
+    x_zero, part, part16 = local_call(
         forward_kernel,
         [
             array((half_width, samples), bf16),
-            array((2 * rank, samples), jnp.float32),
+            array((2 * rank + half_width // 128, samples), jnp.float32),
             array((2 * rank, samples), bf16),
-            array((half_width // 128, 128), jnp.float32),
         ],
         x_rows,
         arrived,
         partner,
-        upstream,
+        hbm(upstream, pltpu.HBM),
         hbm(v_proj, pltpu.HBM),
         hbm(u_proj, pltpu.HBM),
         scalars=1,
@@ -305,26 +303,31 @@
     x_group = lax.all_to_all(
         x_zero.reshape(group, wide, samples), ("y", "c"), split_axis=0, concat_axis=0, tiled=True
     )
-    ranks, message = local_call(
+    message, dx_zero = local_call(
         ranks_kernel,
-        [array((2 * rank, samples), bf16), array((2 * rank + 128, samples), bf16)],
+        [array((2 * rank + 128, samples), bf16), array((half_width, samples), bf16)],
         part,
         other,
-        bias_part,
-        scratch_shapes=[pltpu.VMEM((2 * rank, samples), jnp.float32)],
-        mib=4,
-    )
-
-    mix = dot_first(u_proj, ranks[:rank]) + bias[:, None]
-    cotan = upstream.astype(jnp.float32)
-    dx_zero = (cotan * (mix + 1.0) + dot_first(v_proj, ranks[rank:])).astype(bf16)
+        bias.reshape(-1, CHUNK),
+        hbm(upstream, pltpu.HBM),
+        hbm(v_proj, pltpu.HBM),
+        hbm(u_proj, pltpu.HBM),
+        scratch_shapes=[
+            pltpu.VMEM(upstream.shape, bf16),
+            pltpu.VMEM(v_proj.shape, bf16),
+            pltpu.VMEM(u_proj.shape, bf16),
+            pltpu.VMEM((2 * rank, samples), jnp.float32),
+            pltpu.SemaphoreType.DMA((half_width // CHUNK, 3)),
+        ],
+        specs=[VMEM] * 3 + [pl.BlockSpec(memory_space=pltpu.HBM)] * 3,
+        mib=20,
+    )
     dx_other = lax.ppermute(dx_zero, "t", SWAP)
 
     blocks = [message]
     for k in range(1, ny):
-        blocks.append(shift(blocks[0], "y", ny, k))
-    near_ranks = join_blocks(blocks)
-    far_ranks = lax.ppermute(near_ranks, "c", SWAP)
+        blocks.append(shift(message, "y", ny, k))
+    blocks = blocks + [lax.ppermute(block, "c", SWAP) for block in blocks]
     height = rank // dp_count * (2 * wide // 128) + 2 * wide // 128
     pieces = local_call(
         grads_kernel,
@@ -332,8 +335,7 @@
         jnp.stack([y, c]),
         x_group,
         up_group,
-        near_ranks,
-        far_ranks,
+        *blocks,
         scalars=1,
         scratch_shapes=[
             pltpu.VMEM((rank, 2 * wide), jnp.float32),

time: 195 us -> 205 us (1.051)
  waiting for transfers between devices: 67.7 us -> 76.9 us
  matrix products: 6.09 us -> 0.8 us
  Pallas kernels: 21.5 us -> 24.7 us
  local copies, waits for them, and re-layouts: 3.77 us -> 6.65 us
    ppermute x3, waiting for transfers between devices: 5.62 us -> 19.5 us  [shift(): lax.ppermute(value, axis, [(i, (i + by) % size) for i in range(size)])]
    all_to_all x1, waiting for transfers between devices: 8.03 us -> 0.01 us  [step(): lax.all_to_all(x_zero.reshape(group, wide, samples), ('y', 'c'), split_ax...]
    dot_general x2 -> x0, matrix products: 5.29 us -> none  [dot_first(): lax.dot_general(left, right, (((0,), (0,)), ((), ())), preferred_element_...]
    ppermute x1, waiting for transfers between devices: 2.61 us -> 6.65 us  [step(): other = lax.ppermute(part16, 't', SWAP)]
    pallas_call x5 -> x4, Pallas kernels: 16 us -> 19 us  [local_call(): pl.pallas_call(body, out_shape=out_shape, in_specs=specs or [SMEM] * scal...]
    all_to_all x1, waiting for transfers between devices: 2.07 us -> 0.01 us  [step(): lax.all_to_all(upstream.reshape(group, wide, samples), ('y', 'c'), split_...]
  transfers between devices with their start and end apart: 10 -> 13, of which waited for: 7 -> 5; matrix products, arithmetic and copies ran while one was open for 5% -> 4% of each run, Pallas kernels for 3% -> 9%
where the time goes in v1:
time: 205 us; the launch traced here: 202 us
  waiting for transfers between devices  76.9 us (38%)
  blocking collectives  57 us (28%)
  starting transfers between devices  30.9 us (15%)
  Pallas kernels  24.7 us (12%)
  local copies, waits for them, and re-layouts  6.65 us (3%)
  other arithmetic  3.99 us (2%)
    all_to_all x1, blocking collectives, step(): got = lax.all_to_all(outgoing, DP, split_axis=0, concat_axis=0, tiled=True)  57 us
    all_to_all x1, waiting for transfers between devices, step(): lax.all_to_all(looked, DP, split_axis=1, concat_axis=0, tiled=True)  29.2 us
    ppermute x1, waiting for transfers between devices, step(): partner = lax.ppermute(arrived, 't', SWAP)  21.6 us
    ppermute x3, waiting for transfers between devices, shift(): lax.ppermute(value, axis, [(i, (i + by) % size) for i in range(size)])  19.5 us
    pallas_call x4, Pallas kernels, local_call(): pl.pallas_call(body, out_shape=out_shape, in_specs=specs or [SMEM] * scal...  19 us
    all_to_all x1, starting transfers between devices, step(): lax.all_to_all(looked, DP, split_axis=1, concat_axis=0, tiled=True)  14 us
    ppermute x1, waiting for transfers between devices, step(): other = lax.ppermute(part16, 't', SWAP)  6.65 us
    ppermute x3, starting transfers between devices, shift(): lax.ppermute(value, axis, [(i, (i + by) % size) for i in range(size)])  6.16 us
  transfers between devices with their start and end apart: 13, of which 5 were waited for; matrix products, arithmetic and copies ran while one was open for 4% of the time, Pallas kernels for 9%

profile of v1, /device:TPU:4, one launch (start us, length us, event | category | flops | bytes accessed | tf_op | source)
XLA Modules:
  0.0 201.9 jit_solution(485139238365591802)
XLA Ops:
  0.7 1.2 copy-done
  1.9 1.1 copy_bitcast_fusion
  3.0 14.0 %all-to-all-start = ((bf16[32,128,128]{2,0,1:T(8,128)(2,1)}), bf16[32,128,128]{2,0,1:T(8,128)(2,1)S(1)}, u32[]{:S(2)}, u32[]{:S(2)}) async-start(bf16[32,128,128]{2,0,1:T(8,128)(2,1)} %copy_bitcast_fusion), calls=%async_computation | async-start | bytes 2097152 | tf_op jit(solution)/shard_map/all_to_all | solution.py:267
  17.1 29.2 %all-to-all-done = bf16[32,128,128]{2,0,1:T(8,128)(2,1)S(1)} async-done(((bf16[32,128,128]{2,0,1:T(8,128)(2,1)}), bf16[32,128,128]{2,0,1:T(8,128)(2,1)S(1)}, u32[]{:S(2)}, u32[]{:S(2)}) %all-to-all-start) | async-done | bytes 1048608 | tf_op jit(solution)/shard_map/all_to_all | solution.py:267
  46.2 3.8 %all-to-all-start.2 = ((bf16[8,512,128]{2,1,0:T(8,128)(2,1)}), bf16[8,512,128]{2,1,0:T(8,128)(2,1)S(1)}, u32[]{:S(2)}, u32[]{:S(2)}) async-start(bf16[8,512,128]{2,1,0:T(8,128)(2,1)} %bitcast.20), calls=%async_computation.2 | async-start | bytes 2097152 | tf_op jit(solution)/shard_map/all_to_all | solution.py:269
  50.9 3.8 %fusion.5 = (bf16[8192,128]{1,0:T(8,128)(2,1)S(1)}, bf16[8192,128]{1,0:T(8,128)(2,1)S(1)}) fusion(s32[8192]{0:T(1024)S(1)} %get-tuple-element.23, bf16[8192]{0:T(1024)(128)(2,1)S(1)} %get-tuple-element.26, bf16[8192]{0:T(1024)(128)(2,1)S(1)} %fusion.18), kind=kLoop, calls=%fused_computation.6 | loop fusion | flops 3145728 | bytes 4259840 | tf_op jit(solution)/shard_map/jit(_where)/select_n | solution.py:245
  55.5 21.6 %collective-permute-done.far = bf16[4096,128]{1,0:T(8,128)(2,1)S(1)} collective-permute-done((bf16[4096,128]{1,0:T(8,128)(2,1)S(1)}, bf16[4096,128]{1,0:T(8,128)(2,1)S(1)}, u32[]{:S(2)}, u32[]{:S(2)}) %collective-permute-start) | collective-permute-done | bytes 1048608 | tf_op jit(solution)/shard_map/ppermute | solution.py:268
  77.1 8.1 %shard_map.93 = (bf16[4096,128]{1,0:T(8,128)(2,1)S(1)}, f32[800,128]{1,0:T(8,128)S(1)}, bf16[768,128]{1,0:T(8,128)(2,1)}) custom-call(s32[4096]{0:T(1024)S(1)} %fusion.29.rows, bf16[4096,128]{1,0:T(8,128)(2,1)S(1)} %bitcast.18, bf16[4096,128]{1,0:T(8,128)(2,1)S(1)} %collective-permute-done.far, bf16[4096,128]{1,0:T(8,128)(2,1)} %upstream_in.1, ...), custom_call_target="tpu_custom_call" | custom-call | tf_op jit(solution)/shard_map/pallas_call | solution.py:53
  85.3 1.0 copy-done.1
  86.2 0.8 collective-permute-start.1
  87.7 6.6 %collective-permute-done.1.other = bf16[768,128]{1,0:T(8,128)(2,1)S(1)} collective-permute-done((bf16[768,128]{1,0:T(8,128)(2,1)}, bf16[768,128]{1,0:T(8,128)(2,1)S(1)}, u32[]{:S(2)}, u32[]{:S(2)}) %collective-permute-start.1) | collective-permute-done | bytes 196640 | tf_op jit(solution)/shard_map/ppermute | solution.py:302
  94.4 5.7 %shard_map.94 = (bf16[896,128]{1,0:T(8,128)(2,1)S(1)}, bf16[4096,128]{1,0:T(8,128)(2,1)}) custom-call(f32[800,128]{1,0:T(8,128)S(1)} %get-tuple-element.13.part, bf16[768,128]{1,0:T(8,128)(2,1)S(1)} %collective-permute-done.1.other, f32[8,512]{1,0:T(8,128)S(1)} %reshape.64.bias, bf16[4096,128]{1,0:T(8,128)(2,1)} %upstream_in.1, bf16[384,4096]{1,0:T(8,128)(2,1)} %v_in.1, ...), custom_call_target="tpu_custom_call" | custom-call | tf_op jit(solution)/shard_map/pallas_call | solution.py:53
  101.6 4.0 %all-to-all-start.1 = ((bf16[8,512,128]{2,1,0:T(8,128)(2,1)}), bf16[8,512,128]{2,1,0:T(8,128)(2,1)S(1)}, u32[]{:S(2)}, u32[]{:S(2)}) async-start(bf16[8,512,128]{2,1,0:T(8,128)(2,1)} %bitcast.19), calls=%async_computation.1 | async-start | bytes 2097152 | tf_op jit(solution)/shard_map/all_to_all | solution.py:303
  105.7 2.0 %collective-permute-start.3 = (bf16[896,128]{1,0:T(8,128)(2,1)S(1)}, bf16[896,128]{1,0:T(8,128)(2,1)}, u32[]{:S(2)}, u32[]{:S(2)}) collective-permute-start(bf16[896,128]{1,0:T(8,128)(2,1)S(1)} %copy-done.3), channel_id=1, source_target_pairs={{0,4},{4,8},{8,12},{12,0},{1,5},{5,9},{9,13},{13,1},{2,6},{6,10},{... | collective-permute-start | bytes 688136 | tf_op jit(solution)/shard_map/ppermute | solution.py:28
  107.7 2.7 %collective-permute-start.4 = (bf16[896,128]{1,0:T(8,128)(2,1)S(1)}, bf16[896,128]{1,0:T(8,128)(2,1)}, u32[]{:S(2)}, u32[]{:S(2)}) collective-permute-start(bf16[896,128]{1,0:T(8,128)(2,1)S(1)} %copy-done.3), channel_id=1, source_target_pairs={{0,8},{4,12},{8,0},{12,4},{1,9},{5,13},{9,1},{13,5},{2,10},{6,14},... | collective-permute-start | bytes 688136 | tf_op jit(solution)/shard_map/ppermute | solution.py:28
  110.4 1.5 collective-permute-start.5
  112.1 14.4 %collective-permute-done.3.rest_1_ = bf16[896,128]{1,0:T(8,128)(2,1)} collective-permute-done((bf16[896,128]{1,0:T(8,128)(2,1)S(1)}, bf16[896,128]{1,0:T(8,128)(2,1)}, u32[]{:S(2)}, u32[]{:S(2)}) %collective-permute-start.3) | collective-permute-done | bytes 229408 | tf_op jit(solution)/shard_map/ppermute | solution.py:28
  126.6 5.0 %collective-permute-done.4.rest_2_ = bf16[896,128]{1,0:T(8,128)(2,1)} collective-permute-done((bf16[896,128]{1,0:T(8,128)(2,1)S(1)}, bf16[896,128]{1,0:T(8,128)(2,1)}, u32[]{:S(2)}, u32[]{:S(2)}) %collective-permute-start.4) | collective-permute-done | bytes 229408 | tf_op jit(solution)/shard_map/ppermute | solution.py:28
  132.1 0.8 dynamic-slice_reduce_fusion
  132.9 0.9 reshape.62
  133.9 3.9 %shard_map.95.extra = bf16[128,32,128]{2,1,0:T(8,128)(2,1)S(1)} custom-call(s32[2]{0:T(128)S(1)} %pad_add_fusion.place, bf16[8,512,128]{2,1,0:T(8,128)(2,1)S(1)} %all-to-all-done.1.x_group, bf16[8,512,128]{2,1,0:T(8,128)(2,1)S(1)} %all-to-all-done.2.up_group, bf16[896,128]{1,0:T(8,128)(2,1)S(1)} %copy-done.3, ...), custom_call_target="tpu_custom_call" | custom-call | tf_op jit(solution)/shard_map/pallas_call | solution.py:53
  137.8 5.8 %gather_rows.1 = bf16[128,64,128]{2,1,0:T(8,128)(2,1)S(1)} custom-call(s32[4096]{0:T(1024)S(1)} %fusion.23.rows, bf16[4096,128]{1,0:T(8,128)(2,1)} %get-tuple-element.15.near, bf16[4096,128]{1,0:T(8,128)(2,1)} %collective-permute-done.2.far, bf16[128,32,128]{2,1,0:T(8,128)(2,1)S(1)} %shard_map.95.extra), custom_call_target="tpu_custom_call" | custom-call | tf_op jit(solution)/shard_map/gather_rows/pallas_call | solution.py:87
  143.6 57.0 %all_to_all.34.refs_0_ = bf16[128,64,128]{2,1,0:T(8,128)(2,1)S(1)} all-to-all(bf16[128,64,128]{2,1,0:T(8,128)(2,1)S(1)} %gather_rows.1), channel_id=1, replica_groups=mesh['z'=8,'xl'=2,'y'=4,'c'=2,'t'=2] {'z','xl','y','c'}, dimensions={0} | all-to-all | bytes 4194304 | tf_op jit(solution)/shard_map/all_to_all | solution.py:353
  200.6 1.3 shard_map.96
  (32 shorter events, 4.7 us)
Async XLA Ops:
  0.6 1.2 copy-start
  0.6 16.4 %copy-start.4 = (s32[8192]{0:T(1024)S(1)}, s32[8192]{0:T(1024)}, u32[]{:S(2)}) copy-start(s32[8192]{0:T(1024)} %param.7) | copy-start | bytes 98308
  3.0 43.2 %all-to-all-start = ((bf16[32,128,128]{2,0,1:T(8,128)(2,1)}), bf16[32,128,128]{2,0,1:T(8,128)(2,1)S(1)}, u32[]{:S(2)}, u32[]{:S(2)}) async-start(bf16[32,128,128]{2,0,1:T(8,128)(2,1)} %copy_bitcast_fusion), calls=%async_computation | async-start | bytes 2097152 | tf_op jit(solution)/shard_map/all_to_all | solution.py:267
  46.2 55.4 %all-to-all-start.2 = ((bf16[8,512,128]{2,1,0:T(8,128)(2,1)}), bf16[8,512,128]{2,1,0:T(8,128)(2,1)S(1)}, u32[]{:S(2)}, u32[]{:S(2)}) async-start(bf16[8,512,128]{2,1,0:T(8,128)(2,1)} %bitcast.20), calls=%async_computation.2 | async-start | bytes 2097152 | tf_op jit(solution)/shard_map/all_to_all | solution.py:269
  50.1 27.1 %collective-permute-start = (bf16[4096,128]{1,0:T(8,128)(2,1)S(1)}, bf16[4096,128]{1,0:T(8,128)(2,1)S(1)}, u32[]{:S(2)}, u32[]{:S(2)}) collective-permute-start(bf16[4096,128]{1,0:T(8,128)(2,1)S(1)} %bitcast.17), channel_id=1, source_target_pairs={{0,1},{1,0},{2,3},{3,2},{4,5},{5,4},{6,7},{7,6},{8,9},{9,8},{10,11... | collective-permute-start | bytes 3145736 | tf_op jit(solution)/shard_map/ppermute | solution.py:268
  85.2 1.0 copy-start.1
  86.2 8.2 %collective-permute-start.1 = (bf16[768,128]{1,0:T(8,128)(2,1)}, bf16[768,128]{1,0:T(8,128)(2,1)S(1)}, u32[]{:S(2)}, u32[]{:S(2)}) collective-permute-start(bf16[768,128]{1,0:T(8,128)(2,1)} %get-tuple-element.14), channel_id=1, source_target_pairs={{0,1},{1,0},{2,3},{3,2},{4,5},{5,4},{6,7},{7,6},{8,9},{9,8},{10,11... | collective-permute-start | bytes 589832 | tf_op jit(solution)/shard_map/ppermute | solution.py:302
  100.1 0.7 copy-start.2
  100.8 11.0 %copy-start.5 = (s32[8192]{0:T(1024)S(1)}, s32[8192]{0:T(1024)}, u32[]{:S(2)}) copy-start(s32[8192]{0:T(1024)} %param.7) | copy-start | bytes 98308
  100.8 4.8 %copy-start.3 = (bf16[896,128]{1,0:T(8,128)(2,1)S(1)}, bf16[896,128]{1,0:T(8,128)(2,1)}, u32[]{:S(2)}) copy-start(bf16[896,128]{1,0:T(8,128)(2,1)} %copy-done.2) | copy-start | bytes 688132
  100.8 37.0 %collective-permute-start.2 = (bf16[4096,128]{1,0:T(8,128)(2,1)}, bf16[4096,128]{1,0:T(8,128)(2,1)}, u32[]{:S(2)}, u32[]{:S(2)}) collective-permute-start(bf16[4096,128]{1,0:T(8,128)(2,1)} %get-tuple-element.15.near), channel_id=1, source_target_pairs={{0,1},{1,0},{2,3},{3,2},{4,5},{5,4},{6,7},{7,6},{8,9},{9,8},{10,11... | collective-permute-start | bytes 3145736 | tf_op jit(solution)/shard_map/ppermute | solution.py:325
  101.6 32.3 %all-to-all-start.1 = ((bf16[8,512,128]{2,1,0:T(8,128)(2,1)}), bf16[8,512,128]{2,1,0:T(8,128)(2,1)S(1)}, u32[]{:S(2)}, u32[]{:S(2)}) async-start(bf16[8,512,128]{2,1,0:T(8,128)(2,1)} %bitcast.19), calls=%async_computation.1 | async-start | bytes 2097152 | tf_op jit(solution)/shard_map/all_to_all | solution.py:303
  105.7 20.9 %collective-permute-start.3 = (bf16[896,128]{1,0:T(8,128)(2,1)S(1)}, bf16[896,128]{1,0:T(8,128)(2,1)}, u32[]{:S(2)}, u32[]{:S(2)}) collective-permute-start(bf16[896,128]{1,0:T(8,128)(2,1)S(1)} %copy-done.3), channel_id=1, source_target_pairs={{0,4},{4,8},{8,12},{12,0},{1,5},{5,9},{9,13},{13,1},{2,6},{6,10},{... | collective-permute-start | bytes 688136 | tf_op jit(solution)/shard_map/ppermute | solution.py:28
  107.7 23.9 %collective-permute-start.4 = (bf16[896,128]{1,0:T(8,128)(2,1)S(1)}, bf16[896,128]{1,0:T(8,128)(2,1)}, u32[]{:S(2)}, u32[]{:S(2)}) collective-permute-start(bf16[896,128]{1,0:T(8,128)(2,1)S(1)} %copy-done.3), channel_id=1, source_target_pairs={{0,8},{4,12},{8,0},{12,4},{1,9},{5,13},{9,1},{13,5},{2,10},{6,14},... | collective-permute-start | bytes 688136 | tf_op jit(solution)/shard_map/ppermute | solution.py:28
  110.4 21.2 %collective-permute-start.5 = (bf16[896,128]{1,0:T(8,128)(2,1)S(1)}, bf16[896,128]{1,0:T(8,128)(2,1)}, u32[]{:S(2)}, u32[]{:S(2)}) collective-permute-start(bf16[896,128]{1,0:T(8,128)(2,1)S(1)} %copy-done.3), channel_id=1, source_target_pairs={{0,12},{4,0},{8,4},{12,8},{1,13},{5,1},{9,5},{13,9},{2,14},{6,2},{... | collective-permute-start | bytes 688136 | tf_op jit(solution)/shard_map/ppermute | solution.py:28
  112.1 21.8 %collective-permute-start.6 = (bf16[896,128]{1,0:T(8,128)(2,1)S(1)}, bf16[896,128]{1,0:T(8,128)(2,1)}, u32[]{:S(2)}, u32[]{:S(2)}) collective-permute-start(bf16[896,128]{1,0:T(8,128)(2,1)S(1)} %copy-done.3), channel_id=1, source_target_pairs={{0,2},{2,0},{1,3},{3,1},{4,6},{6,4},{5,7},{7,5},{8,10},{10,8},{9,1... | collective-permute-start | bytes 688136 | tf_op jit(solution)/shard_map/ppermute | solution.py:330
  126.5 7.3 %collective-permute-start.7 = (bf16[896,128]{1,0:T(8,128)(2,1)}, bf16[896,128]{1,0:T(8,128)(2,1)}, u32[]{:S(2)}, u32[]{:S(2)}) collective-permute-start(bf16[896,128]{1,0:T(8,128)(2,1)} %collective-permute-done.3.rest_1_), channel_id=1, source_target_pairs={{0,2},{2,0},{1,3},{3,1},{4,6},{6,4},{5,7},{7,5},{8,10},{10,8},{9,1... | collective-permute-start | bytes 688136 | tf_op jit(solution)/shard_map/ppermute | solution.py:330
  131.6 2.3 %collective-permute-start.8 = (bf16[896,128]{1,0:T(8,128)(2,1)}, bf16[896,128]{1,0:T(8,128)(2,1)}, u32[]{:S(2)}, u32[]{:S(2)}) collective-permute-start(bf16[896,128]{1,0:T(8,128)(2,1)} %collective-permute-done.4.rest_2_), channel_id=1, source_target_pairs={{0,2},{2,0},{1,3},{3,1},{4,6},{6,4},{5,7},{7,5},{8,10},{10,8},{9,1... | collective-permute-start | bytes 688136 | tf_op jit(solution)/shard_map/ppermute | solution.py:330
  131.6 2.3 %collective-permute-start.9 = (bf16[896,128]{1,0:T(8,128)(2,1)}, bf16[896,128]{1,0:T(8,128)(2,1)}, u32[]{:S(2)}, u32[]{:S(2)}) collective-permute-start(bf16[896,128]{1,0:T(8,128)(2,1)} %collective-permute-done.5.rest_3_), channel_id=1, source_target_pairs={{0,2},{2,0},{1,3},{3,1},{4,6},{6,4},{5,7},{7,5},{8,10},{10,8},{9,1... | collective-permute-start | bytes 688136 | tf_op jit(solution)/shard_map/ppermute | solution.py:330

commit v2 on v1

--- a/solution.py
+++ b/solution.py
@@ -16,11 +16,18 @@
 
 SMEM = pl.BlockSpec(memory_space=pltpu.SMEM)
 VMEM = pl.BlockSpec(memory_space=pltpu.VMEM)
+HBM = pl.BlockSpec(memory_space=pltpu.HBM)
 
 
 def dot_last(left, right):
     return lax.dot_general(
         left, right, (((1,), (1,)), ((), ())), preferred_element_type=jnp.float32
+    )
+
+
+def dot_first(left, right):
+    return lax.dot_general(
+        left, right, (((0,), (0,)), ((), ())), preferred_element_type=jnp.float32
     )
 
 
@@ -70,15 +77,31 @@
     lax.fori_loop(0, picked.shape[0] // UNROLL, step, 0)
 
 
-def gather_kernel(rows, near, far, extra, out, table, picked):
+def start_copies(pairs, sems):
+    copies = [pltpu.make_async_copy(a, b, sems.at[i]) for i, (a, b) in enumerate(pairs)]
+    for copy in copies:
+        copy.start()
+    return copies
+
+
+def in_hbm(*values):
+    return [pltpu.with_memory_space_constraint(value, pltpu.HBM) for value in values]
+
+
+def gather_kernel(rows_in, near_in, far_in, extra, out, rows, near, far, table, picked, sems):
     half = near.shape[0]
     dests, height, lanes = out.shape
     block = height - extra.shape[1]
+    pairs = ((near_in, near), (far_in, far), (rows_in, rows), (extra, out.at[:, block:, :]))
+    copies = start_copies(pairs, sems)
+    copies[0].wait()
     table[:half] = near[...].astype(jnp.float32)
+    copies[1].wait()
     table[half:] = far[...].astype(jnp.float32)
+    copies[2].wait()
     pick_rows(rows, table, picked)
     out[:, :block, :] = picked[...].reshape(dests, block, lanes).astype(out.dtype)
-    out[:, block:, :] = extra[...]
+    copies[3].wait()
 
 
 def gather(rows, near, far, extra):
@@ -87,29 +110,33 @@
     return pl.pallas_call(
         gather_kernel,
         out_shape=jax.ShapeDtypeStruct((dests, count // dests + height, lanes), near.dtype),
-        in_specs=[SMEM, VMEM, VMEM, VMEM],
+        in_specs=[HBM] * 3 + [VMEM],
         out_specs=VMEM,
         scratch_shapes=[
+            pltpu.SMEM((count,), jnp.int32),
+            pltpu.VMEM(near.shape, near.dtype),
+            pltpu.VMEM(far.shape, far.dtype),
             pltpu.VMEM((2 * near.shape[0], lanes), jnp.float32),
             pltpu.VMEM((count, lanes), jnp.float32),
+            pltpu.SemaphoreType.DMA((4,)),
         ],
         compiler_params=pltpu.CompilerParams(vmem_limit_bytes=16 * 2**20),
         name="gather_rows",
-    )(rows, near, far, extra)
-
-
-def forward_kernel(rows, near, far, *rest):
-    sources, (x_out, part, part16, table, picked, *copied, sems) = rest[:3], rest[3:]
-    copies = [pltpu.make_async_copy(a, b, sems.at[i]) for i, (a, b) in enumerate(zip(sources, copied))]
-    for copy in copies:
-        copy.start()
-    upstream, v_proj, u_proj = copied
+    )(*in_hbm(rows, near, far), extra)
+
+
+def forward_kernel(near, *rest):
+    sources, (x_out, part, part16, table, picked, *copied, sems) = rest[:5], rest[5:]
+    copies = start_copies(zip(sources, copied), sems)
+    rows, far, upstream, v_proj, u_proj = copied
     half, lanes = near.shape
     rank = v_proj.shape[0]
     table[:half] = near[...].astype(jnp.float32)
+    copies[1].wait()
     table[half:] = far[...].astype(jnp.float32)
+    copies[0].wait()
     pick_rows(rows, table, picked)
-    for copy in copies:
+    for copy in copies[2:]:
         copy.wait()
     ones = jnp.ones((8, 3 * lanes), jnp.bfloat16)
     h_sum = jnp.zeros((rank, lanes), jnp.float32)
@@ -134,22 +161,11 @@
     part16[rank:] = d_sum.astype(jnp.bfloat16)
 
 
-def ranks_kernel(part, other, bias, upstream_in, v_in, u_in, message, dx, upstream, v_proj, u_proj, total, sems):
+def ranks_kernel(part, other, ranks, message, total):
     rows = other.shape[0]
     rank = rows // 2
-    count = upstream.shape[0] // CHUNK
-    copies = []
-    for k in range(count):
-        here = slice(k * CHUNK, (k + 1) * CHUNK)
-        pairs = (
-            (u_in.at[:, here], u_proj.at[:, here]),
-            (v_in.at[:, here], v_proj.at[:, here]),
-            (upstream_in.at[here], upstream.at[here]),
-        )
-        copies.append([pltpu.make_async_copy(a, b, sems.at[k, i]) for i, (a, b) in enumerate(pairs)])
-        for copy in copies[-1]:
-            copy.start()
     value = part[:rows] + other[...].astype(jnp.float32)
+    ranks[...] = value.astype(jnp.bfloat16)
     total[...] = value
     step = rank // 128
     for i in range(2):
@@ -158,16 +174,6 @@
             rank_rows = total[pl.ds(i * rank + j, 128, stride=step), :]
             message[to : to + 128, :] = rank_rows.astype(jnp.bfloat16)
     store3(message, rows, part[rows:])
-    h_turned = value[:rank].T.astype(jnp.bfloat16)
-    d_turned = value[rank:].T.astype(jnp.bfloat16)
-    for k in range(count):
-        here = slice(k * CHUNK, (k + 1) * CHUNK)
-        for copy in copies[k]:
-            copy.wait()
-        mix = jnp.dot(h_turned, u_proj[:, here], preferred_element_type=jnp.float32)
-        mix = (mix + bias[k : k + 1, :]).T
-        back = jnp.dot(d_turned, v_proj[:, here], preferred_element_type=jnp.float32).T
-        dx[here, :] = (upstream[here, :].astype(jnp.float32) * (mix + 1.0) + back).astype(jnp.bfloat16)
 
 
 def grads_kernel(place, x_group, up_group, *rest):
@@ -273,7 +279,6 @@
     side = wire // block_rows % 2
     spot = wire // (2 * block_rows) * block_rows + wire % block_rows
     x_rows = jnp.where(side == t, 0, half_width) + spot
-    hbm = pltpu.with_memory_space_constraint
     x_zero, part, part16 = local_call(
         forward_kernel,
         [
@@ -281,47 +286,36 @@
             array((2 * rank + half_width // 128, samples), jnp.float32),
             array((2 * rank, samples), bf16),
         ],
-        x_rows,
         arrived,
-        partner,
-        hbm(upstream, pltpu.HBM),
-        hbm(v_proj, pltpu.HBM),
-        hbm(u_proj, pltpu.HBM),
-        scalars=1,
+        *in_hbm(x_rows, partner, upstream, v_proj, u_proj),
         scratch_shapes=[
             pltpu.VMEM((2 * half_width, samples), jnp.float32),
             pltpu.VMEM((half_width, samples), jnp.float32),
+            pltpu.SMEM(x_rows.shape, jnp.int32),
+            pltpu.VMEM(partner.shape, bf16),
             pltpu.VMEM(upstream.shape, bf16),
             pltpu.VMEM(v_proj.shape, bf16),
             pltpu.VMEM(u_proj.shape, bf16),
-            pltpu.SemaphoreType.DMA((3,)),
-        ],
-        specs=[SMEM, VMEM, VMEM] + [pl.BlockSpec(memory_space=pltpu.HBM)] * 3,
+            pltpu.SemaphoreType.DMA((5,)),
+        ],
+        specs=[VMEM] + [HBM] * 5,
         mib=28,
     )
     other = lax.ppermute(part16, "t", SWAP)
     x_group = lax.all_to_all(
         x_zero.reshape(group, wide, samples), ("y", "c"), split_axis=0, concat_axis=0, tiled=True
     )
-    message, dx_zero = local_call(
+    ranks, message = local_call(
         ranks_kernel,
-        [array((2 * rank + 128, samples), bf16), array((half_width, samples), bf16)],
+        [array((2 * rank, samples), bf16), array((2 * rank + 128, samples), bf16)],
         part,
         other,
-        bias.reshape(-1, CHUNK),
-        hbm(upstream, pltpu.HBM),
-        hbm(v_proj, pltpu.HBM),
-        hbm(u_proj, pltpu.HBM),
-        scratch_shapes=[
-            pltpu.VMEM(upstream.shape, bf16),
-            pltpu.VMEM(v_proj.shape, bf16),
-            pltpu.VMEM(u_proj.shape, bf16),
-            pltpu.VMEM((2 * rank, samples), jnp.float32),
-            pltpu.SemaphoreType.DMA((half_width // CHUNK, 3)),
-        ],
-        specs=[VMEM] * 3 + [pl.BlockSpec(memory_space=pltpu.HBM)] * 3,
-        mib=20,
-    )
+        scratch_shapes=[pltpu.VMEM((2 * rank, samples), jnp.float32)],
+        mib=4,
+    )
+    mix = dot_first(u_proj, ranks[:rank]) + bias[:, None]
+    cotan = upstream.astype(jnp.float32)
+    dx_zero = (cotan * (mix + 1.0) + dot_first(v_proj, ranks[rank:])).astype(bf16)
     dx_other = lax.ppermute(dx_zero, "t", SWAP)
 
     blocks = [message]

time: 205 us -> 206 us (level)
  matrix products: 0.8 us -> 7.07 us
  Pallas kernels: 24.7 us -> 18.6 us
    dot_general x0 -> x2, matrix products: none -> 6.27 us  [dot_first(): lax.dot_general(left, right, (((0,), (0,)), ((), ())), preferred_element_...]
    all_to_all x1, waiting for transfers between devices: 0.01 us -> 6.13 us  [step(): lax.all_to_all(upstream.reshape(group, wide, samples), ('y', 'c'), split_...]
    pallas_call x4, Pallas kernels: 19 us -> 13 us  [local_call(): pl.pallas_call(body, out_shape=out_shape, in_specs=specs or [SMEM] * scal...]
    ppermute x1, waiting for transfers between devices: 6.65 us -> 2.6 us  [step(): other = lax.ppermute(part16, 't', SWAP)]
  transfers between devices with their start and end apart: 13 -> 13, of which waited for: 5 -> 6; matrix products, arithmetic and copies ran while one was open for 4% -> 7% of each run, Pallas kernels for 9% -> 2%
where the time goes in v2:
time: 206 us; the launch traced here: 203 us
  waiting for transfers between devices  77 us (37%)
  blocking collectives  57.8 us (28%)
  starting transfers between devices  30.3 us (15%)
  Pallas kernels  18.6 us (9%)
  matrix products  7.07 us (3%)
  local copies, waits for them, and re-layouts  6.2 us (3%)
  other arithmetic  5.2 us (3%)
    all_to_all x1, blocking collectives, step(): got = lax.all_to_all(outgoing, DP, split_axis=0, concat_axis=0, tiled=True)  57.8 us
    all_to_all x1, waiting for transfers between devices, step(): lax.all_to_all(looked, DP, split_axis=1, concat_axis=0, tiled=True)  29.2 us
    ppermute x1, waiting for transfers between devices, step(): partner = lax.ppermute(arrived, 't', SWAP)  19.6 us
    ppermute x3, waiting for transfers between devices, shift(): lax.ppermute(value, axis, [(i, (i + by) % size) for i in range(size)])  19.5 us
    all_to_all x1, starting transfers between devices, step(): lax.all_to_all(looked, DP, split_axis=1, concat_axis=0, tiled=True)  14 us
    pallas_call x4, Pallas kernels, local_call(): pl.pallas_call(body, out_shape=out_shape, in_specs=specs or [SMEM] * scal...  13 us
    dot_general x2, matrix products, dot_first(): lax.dot_general(left, right, (((0,), (0,)), ((), ())), preferred_element_...  6.27 us
    all_to_all x1, waiting for transfers between devices, step(): lax.all_to_all(upstream.reshape(group, wide, samples), ('y', 'c'), split_...  6.13 us
  transfers between devices with their start and end apart: 13, of which 6 were waited for; matrix products, arithmetic and copies ran while one was open for 7% of the time, Pallas kernels for 2%

profile of v2, /device:TPU:4, one launch (start us, length us, event | category | flops | bytes accessed | tf_op | source)
XLA Modules:
  0.0 203.0 jit_solution(14750604328014467905)
XLA Ops:
  0.7 1.2 copy-done
  1.9 1.1 copy_bitcast_fusion
  3.0 14.0 %all-to-all-start = ((bf16[32,128,128]{2,0,1:T(8,128)(2,1)}), bf16[32,128,128]{2,0,1:T(8,128)(2,1)S(1)}, u32[]{:S(2)}, u32[]{:S(2)}) async-start(bf16[32,128,128]{2,0,1:T(8,128)(2,1)} %copy_bitcast_fusion), calls=%async_computation | async-start | bytes 2097152 | tf_op jit(solution)/shard_map/all_to_all | solution.py:273
  17.1 29.2 %all-to-all-done = bf16[32,128,128]{2,0,1:T(8,128)(2,1)S(1)} async-done(((bf16[32,128,128]{2,0,1:T(8,128)(2,1)}), bf16[32,128,128]{2,0,1:T(8,128)(2,1)S(1)}, u32[]{:S(2)}, u32[]{:S(2)}) %all-to-all-start) | async-done | bytes 1048608 | tf_op jit(solution)/shard_map/all_to_all | solution.py:273
  47.1 3.8 %fusion.10 = (bf16[8192,128]{1,0:T(8,128)(2,1)S(1)}, bf16[8192,128]{1,0:T(8,128)(2,1)S(1)}) fusion(s32[8192]{0:T(1024)S(1)} %get-tuple-element.23, bf16[8192]{0:T(1024)(128)(2,1)S(1)} %get-tuple-element.26, bf16[8192]{0:T(1024)(128)(2,1)S(1)} %fusion.25), kind=kLoop, calls=%fused_computation.13 | loop fusion | flops 3145728 | bytes 4259840 | tf_op jit(solution)/shard_map/jit(_where)/select_n | solution.py:251
  52.3 19.6 %collective-permute-done.rest_1_ = bf16[4096,128]{1,0:T(8,128)(2,1)S(1)} collective-permute-done((bf16[4096,128]{1,0:T(8,128)(2,1)S(1)}, bf16[4096,128]{1,0:T(8,128)(2,1)S(1)}, u32[]{:S(2)}, u32[]{:S(2)}) %collective-permute-start) | collective-permute-done | bytes 1048608 | tf_op jit(solution)/shard_map/ppermute | solution.py:274
  72.0 1.0 copy-done.3
  72.9 7.7 %shard_map.93 = (bf16[4096,128]{1,0:T(8,128)(2,1)S(1)}, f32[800,128]{1,0:T(8,128)S(1)}, bf16[768,128]{1,0:T(8,128)(2,1)S(1)}) custom-call(bf16[4096,128]{1,0:T(8,128)(2,1)S(1)} %bitcast.30, s32[4096]{0:T(1024)} %fusion.36.rest_0_, bf16[4096,128]{1,0:T(8,128)(2,1)} %copy-done.3, bf16[4096,128]{1,0:T(8,128)(2,1)} %rest_2_.1, bf16[384,4096]{1,0:T(8,128)(2,1)} %rest_3_.1, ...), custom_call_target="tpu_custom_call" | custom-call | tf_op jit(solution)/shard_map/pallas_call | solution.py:60
  80.7 1.0 copy-done.1
  82.5 3.8 %all-to-all-start.2 = ((bf16[8,512,128]{2,1,0:T(8,128)(2,1)}), bf16[8,512,128]{2,1,0:T(8,128)(2,1)S(1)}, u32[]{:S(2)}, u32[]{:S(2)}) async-start(bf16[8,512,128]{2,1,0:T(8,128)(2,1)} %bitcast.32), calls=%async_computation.2 | async-start | bytes 2097152 | tf_op jit(solution)/shard_map/all_to_all | solution.py:275
  86.2 2.6 %collective-permute-done.1.other = bf16[768,128]{1,0:T(8,128)(2,1)S(1)} collective-permute-done((bf16[768,128]{1,0:T(8,128)(2,1)S(1)}, bf16[768,128]{1,0:T(8,128)(2,1)S(1)}, u32[]{:S(2)}, u32[]{:S(2)}) %collective-permute-start.1) | collective-permute-done | bytes 196640 | tf_op jit(solution)/shard_map/ppermute | solution.py:304
  88.9 3.8 %fusion.3 = f32[4096,128]{1,0:T(8,128)S(1)} fusion(bf16[384,4096]{1,0:T(8,128)(2,1)} %rest_4_.1, bf16[4096,128]{1,0:T(8,128)(2,1)} %rest_2_.1, f32[4096]{0:T(1024)S(1)} %copy-done.5, bf16[768,128]{1,0:T(8,128)(2,1)S(1)} %get-tuple-element.15), kind=kOutput, calls=%fused_computation.5 | convolution fusion | flops 404750336 | bytes 6406144 | tf_op jit(solution)/shard_map/dot_general | solution.py:29
  92.8 2.4 %fusion.4.near_in = bf16[4096,128]{1,0:T(8,128)(2,1)} fusion(f32[4096,128]{1,0:T(8,128)S(1)} %fusion.3, bf16[384,4096]{1,0:T(8,128)(2,1)S(1)} %copy-done.2, bf16[768,128]{1,0:T(8,128)(2,1)S(1)} %get-tuple-element.15), kind=kOutput, calls=%fused_computation.6 | convolution fusion | flops 403701760 | bytes 6389760 | tf_op jit(solution)/shard_map/dot_general | solution.py:29
  96.0 6.1 %all-to-all-done.2.up_group = bf16[8,512,128]{2,1,0:T(8,128)(2,1)S(1)} async-done(((bf16[8,512,128]{2,1,0:T(8,128)(2,1)}), bf16[8,512,128]{2,1,0:T(8,128)(2,1)S(1)}, u32[]{:S(2)}, u32[]{:S(2)}) %all-to-all-start.2) | async-done | bytes 1048608 | tf_op jit(solution)/shard_map/all_to_all | solution.py:275
  102.2 3.6 %all-to-all-start.1 = ((bf16[8,512,128]{2,1,0:T(8,128)(2,1)}), bf16[8,512,128]{2,1,0:T(8,128)(2,1)S(1)}, u32[]{:S(2)}, u32[]{:S(2)}) async-start(bf16[8,512,128]{2,1,0:T(8,128)(2,1)} %bitcast.31), calls=%async_computation.1 | async-start | bytes 2097152 | tf_op jit(solution)/shard_map/all_to_all | solution.py:305
  105.7 1.9 collective-permute-start.3
  107.7 2.7 %collective-permute-start.4 = (bf16[896,128]{1,0:T(8,128)(2,1)S(1)}, bf16[896,128]{1,0:T(8,128)(2,1)}, u32[]{:S(2)}, u32[]{:S(2)}) collective-permute-start(bf16[896,128]{1,0:T(8,128)(2,1)S(1)} %get-tuple-element.17.rest_0_), channel_id=1, source_target_pairs={{0,8},{4,12},{8,0},{12,4},{1,9},{5,13},{9,1},{13,5},{2,10},{6,14},... | collective-permute-start | bytes 688136 | tf_op jit(solution)/shard_map/ppermute | solution.py:35
  110.4 1.4 collective-permute-start.5
  112.1 14.5 %collective-permute-done.3.rest_1_ = bf16[896,128]{1,0:T(8,128)(2,1)} collective-permute-done((bf16[896,128]{1,0:T(8,128)(2,1)S(1)}, bf16[896,128]{1,0:T(8,128)(2,1)}, u32[]{:S(2)}, u32[]{:S(2)}) %collective-permute-start.3) | collective-permute-done | bytes 229408 | tf_op jit(solution)/shard_map/ppermute | solution.py:35
  126.6 5.0 %collective-permute-done.4.rest_2_ = bf16[896,128]{1,0:T(8,128)(2,1)} collective-permute-done((bf16[896,128]{1,0:T(8,128)(2,1)S(1)}, bf16[896,128]{1,0:T(8,128)(2,1)}, u32[]{:S(2)}, u32[]{:S(2)}) %collective-permute-start.4) | collective-permute-done | bytes 229408 | tf_op jit(solution)/shard_map/ppermute | solution.py:35
  134.5 3.9 %shard_map.95.extra = bf16[128,32,128]{2,1,0:T(8,128)(2,1)S(1)} custom-call(s32[2]{0:T(128)S(1)} %pad_add_fusion.place, bf16[8,512,128]{2,1,0:T(8,128)(2,1)S(1)} %all-to-all-done.1.x_group, bf16[8,512,128]{2,1,0:T(8,128)(2,1)S(1)} %all-to-all-done.2.up_group, bf16[896,128]{1,0:T(8,128)(2,1)S(1)} %get-tuple-element.17.rest_0_, ...), custom_call_target="tpu_custom_call" | custom-call | tf_op jit(solution)/shard_map/pallas_call | solution.py:60
  138.4 5.6 %gather_rows.1 = bf16[128,64,128]{2,1,0:T(8,128)(2,1)S(1)} custom-call(s32[4096]{0:T(1024)} %fusion.30.rows_in, bf16[4096,128]{1,0:T(8,128)(2,1)} %fusion.4.near_in, bf16[4096,128]{1,0:T(8,128)(2,1)} %collective-permute-done.2.far_in, bf16[128,32,128]{2,1,0:T(8,128)(2,1)S(1)} %shard_map.95.extra), custom_call_target="tpu_custom_call" | custom-call | tf_op jit(solution)/shard_map/gather_rows/pallas_call | solution.py:110
  144.0 57.8 %all_to_all.34.refs_0_ = bf16[128,64,128]{2,1,0:T(8,128)(2,1)S(1)} all-to-all(bf16[128,64,128]{2,1,0:T(8,128)(2,1)S(1)} %gather_rows.1), channel_id=1, replica_groups=mesh['z'=8,'xl'=2,'y'=4,'c'=2,'t'=2] {'z','xl','y','c'}, dimensions={0} | all-to-all | bytes 4194304 | tf_op jit(solution)/shard_map/all_to_all | solution.py:347
  201.7 1.3 shard_map.96
  (33 shorter events, 7.2 us)
Async XLA Ops:
  0.6 1.2 copy-start
  0.6 16.4 %copy-start.4 = (s32[8192]{0:T(1024)S(1)}, s32[8192]{0:T(1024)}, u32[]{:S(2)}) copy-start(s32[8192]{0:T(1024)} %param.7) | copy-start | bytes 98308
  3.0 43.2 %all-to-all-start = ((bf16[32,128,128]{2,0,1:T(8,128)(2,1)}), bf16[32,128,128]{2,0,1:T(8,128)(2,1)S(1)}, u32[]{:S(2)}, u32[]{:S(2)}) async-start(bf16[32,128,128]{2,0,1:T(8,128)(2,1)} %copy_bitcast_fusion), calls=%async_computation | async-start | bytes 2097152 | tf_op jit(solution)/shard_map/all_to_all | solution.py:273
  46.3 25.7 %collective-permute-start = (bf16[4096,128]{1,0:T(8,128)(2,1)S(1)}, bf16[4096,128]{1,0:T(8,128)(2,1)S(1)}, u32[]{:S(2)}, u32[]{:S(2)}) collective-permute-start(bf16[4096,128]{1,0:T(8,128)(2,1)S(1)} %bitcast.29), channel_id=1, source_target_pairs={{0,1},{1,0},{2,3},{3,2},{4,5},{5,4},{6,7},{7,6},{8,9},{9,8},{10,11... | collective-permute-start | bytes 3145736 | tf_op jit(solution)/shard_map/ppermute | solution.py:274
  72.0 1.0 copy-start.3
  80.7 1.0 copy-start.1
  81.6 7.3 %copy-start.5 = (f32[4096]{0:T(1024)S(1)}, f32[4096]{0:T(1024)}, u32[]{:S(2)}) copy-start(f32[4096]{0:T(1024)} %param.10) | copy-start | bytes 49156
  81.7 7.2 %collective-permute-start.1 = (bf16[768,128]{1,0:T(8,128)(2,1)S(1)}, bf16[768,128]{1,0:T(8,128)(2,1)S(1)}, u32[]{:S(2)}, u32[]{:S(2)}) collective-permute-start(bf16[768,128]{1,0:T(8,128)(2,1)S(1)} %get-tuple-element.14), channel_id=1, source_target_pairs={{0,1},{1,0},{2,3},{3,2},{4,5},{5,4},{6,7},{7,6},{8,9},{9,8},{10,11... | collective-permute-start | bytes 589832 | tf_op jit(solution)/shard_map/ppermute | solution.py:304
  82.5 19.7 %all-to-all-start.2 = ((bf16[8,512,128]{2,1,0:T(8,128)(2,1)}), bf16[8,512,128]{2,1,0:T(8,128)(2,1)S(1)}, u32[]{:S(2)}, u32[]{:S(2)}) async-start(bf16[8,512,128]{2,1,0:T(8,128)(2,1)} %bitcast.32), calls=%async_computation.2 | async-start | bytes 2097152 | tf_op jit(solution)/shard_map/all_to_all | solution.py:275
  88.9 3.9 %copy-start.2 = (bf16[384,4096]{1,0:T(8,128)(2,1)S(1)}, bf16[384,4096]{1,0:T(8,128)(2,1)}, u32[]{:S(2)}) copy-start(bf16[384,4096]{1,0:T(8,128)(2,1)} %rest_3_.1) | copy-start | bytes 9437188
  95.2 43.1 %collective-permute-start.2 = (bf16[4096,128]{1,0:T(8,128)(2,1)}, bf16[4096,128]{1,0:T(8,128)(2,1)}, u32[]{:S(2)}, u32[]{:S(2)}) collective-permute-start(bf16[4096,128]{1,0:T(8,128)(2,1)} %fusion.4.near_in), channel_id=1, source_target_pairs={{0,1},{1,0},{2,3},{3,2},{4,5},{5,4},{6,7},{7,6},{8,9},{9,8},{10,11... | collective-permute-start | bytes 3145736 | tf_op jit(solution)/shard_map/ppermute | solution.py:319
  102.2 32.3 %all-to-all-start.1 = ((bf16[8,512,128]{2,1,0:T(8,128)(2,1)}), bf16[8,512,128]{2,1,0:T(8,128)(2,1)S(1)}, u32[]{:S(2)}, u32[]{:S(2)}) async-start(bf16[8,512,128]{2,1,0:T(8,128)(2,1)} %bitcast.31), calls=%async_computation.1 | async-start | bytes 2097152 | tf_op jit(solution)/shard_map/all_to_all | solution.py:305
  105.7 20.8 %collective-permute-start.3 = (bf16[896,128]{1,0:T(8,128)(2,1)S(1)}, bf16[896,128]{1,0:T(8,128)(2,1)}, u32[]{:S(2)}, u32[]{:S(2)}) collective-permute-start(bf16[896,128]{1,0:T(8,128)(2,1)S(1)} %get-tuple-element.17.rest_0_), channel_id=1, source_target_pairs={{0,4},{4,8},{8,12},{12,0},{1,5},{5,9},{9,13},{13,1},{2,6},{6,10},{... | collective-permute-start | bytes 688136 | tf_op jit(solution)/shard_map/ppermute | solution.py:35
  107.7 23.9 %collective-permute-start.4 = (bf16[896,128]{1,0:T(8,128)(2,1)S(1)}, bf16[896,128]{1,0:T(8,128)(2,1)}, u32[]{:S(2)}, u32[]{:S(2)}) collective-permute-start(bf16[896,128]{1,0:T(8,128)(2,1)S(1)} %get-tuple-element.17.rest_0_), channel_id=1, source_target_pairs={{0,8},{4,12},{8,0},{12,4},{1,9},{5,13},{9,1},{13,5},{2,10},{6,14},... | collective-permute-start | bytes 688136 | tf_op jit(solution)/shard_map/ppermute | solution.py:35
  110.4 21.2 %collective-permute-start.5 = (bf16[896,128]{1,0:T(8,128)(2,1)S(1)}, bf16[896,128]{1,0:T(8,128)(2,1)}, u32[]{:S(2)}, u32[]{:S(2)}) collective-permute-start(bf16[896,128]{1,0:T(8,128)(2,1)S(1)} %get-tuple-element.17.rest_0_), channel_id=1, source_target_pairs={{0,12},{4,0},{8,4},{12,8},{1,13},{5,1},{9,5},{13,9},{2,14},{6,2},{... | collective-permute-start | bytes 688136 | tf_op jit(solution)/shard_map/ppermute | solution.py:35
  112.0 22.4 %collective-permute-start.6 = (bf16[896,128]{1,0:T(8,128)(2,1)S(1)}, bf16[896,128]{1,0:T(8,128)(2,1)}, u32[]{:S(2)}, u32[]{:S(2)}) collective-permute-start(bf16[896,128]{1,0:T(8,128)(2,1)S(1)} %get-tuple-element.17.rest_0_), channel_id=1, source_target_pairs={{0,2},{2,0},{1,3},{3,1},{4,6},{6,4},{5,7},{7,5},{8,10},{10,8},{9,1... | collective-permute-start | bytes 688136 | tf_op jit(solution)/shard_map/ppermute | solution.py:324
  126.6 7.9 %collective-permute-start.7 = (bf16[896,128]{1,0:T(8,128)(2,1)}, bf16[896,128]{1,0:T(8,128)(2,1)}, u32[]{:S(2)}, u32[]{:S(2)}) collective-permute-start(bf16[896,128]{1,0:T(8,128)(2,1)} %collective-permute-done.3.rest_1_), channel_id=1, source_target_pairs={{0,2},{2,0},{1,3},{3,1},{4,6},{6,4},{5,7},{7,5},{8,10},{10,8},{9,1... | collective-permute-start | bytes 688136 | tf_op jit(solution)/shard_map/ppermute | solution.py:324
  131.6 2.9 %collective-permute-start.8 = (bf16[896,128]{1,0:T(8,128)(2,1)}, bf16[896,128]{1,0:T(8,128)(2,1)}, u32[]{:S(2)}, u32[]{:S(2)}) collective-permute-start(bf16[896,128]{1,0:T(8,128)(2,1)} %collective-permute-done.4.rest_2_), channel_id=1, source_target_pairs={{0,2},{2,0},{1,3},{3,1},{4,6},{6,4},{5,7},{7,5},{8,10},{10,8},{9,1... | collective-permute-start | bytes 688136 | tf_op jit(solution)/shard_map/ppermute | solution.py:324
  131.6 2.9 %collective-permute-start.9 = (bf16[896,128]{1,0:T(8,128)(2,1)}, bf16[896,128]{1,0:T(8,128)(2,1)}, u32[]{:S(2)}, u32[]{:S(2)}) collective-permute-start(bf16[896,128]{1,0:T(8,128)(2,1)} %collective-permute-done.5.rest_3_), channel_id=1, source_target_pairs={{0,2},{2,0},{1,3},{3,1},{4,6},{6,4},{5,7},{7,5},{8,10},{10,8},{9,1... | collective-permute-start | bytes 688136 | tf_op jit(solution)/shard_map/ppermute | solution.py:324

commit v3 on v0

--- a/solution.py
+++ b/solution.py
@@ -16,11 +16,12 @@
 
 SMEM = pl.BlockSpec(memory_space=pltpu.SMEM)
 VMEM = pl.BlockSpec(memory_space=pltpu.VMEM)
-
-
-def dot_last(left, right, precision=None):
+HBM = pl.BlockSpec(memory_space=pltpu.HBM)
+
+
+def dot_last(left, right):
     return lax.dot_general(
-        left, right, (((1,), (1,)), ((), ())), precision=precision, preferred_element_type=jnp.float32
+        left, right, (((1,), (1,)), ((), ())), preferred_element_type=jnp.float32
     )
 
 
@@ -104,20 +105,31 @@
     )(rows, near, far, extra)
 
 
-def forward_kernel(rows, near, far, *rest):
-    sources, (x_out, part, part16, bias_out, table, picked, *copied, sems) = rest[:3], rest[3:]
-    copies = [pltpu.make_async_copy(a, b, sems.at[i]) for i, (a, b) in enumerate(zip(sources, copied))]
+def start_copies(pairs, sems):
+    copies = [pltpu.make_async_copy(a, b, sems.at[i]) for i, (a, b) in enumerate(pairs)]
     for copy in copies:
         copy.start()
-    upstream, v_proj, u_proj = copied
+    return copies
+
+
+def in_hbm(*values):
+    return [pltpu.with_memory_space_constraint(value, pltpu.HBM) for value in values]
+
+
+def forward_kernel(near, *rest):
+    sources, (x_out, part, part16, table, picked, *copied, sems) = rest[:5], rest[5:]
+    copies = start_copies(zip(sources, copied), sems)
+    rows, far, upstream, v_proj, u_proj = copied
     half, lanes = near.shape
     rank = v_proj.shape[0]
     table[:half] = near[...].astype(jnp.float32)
+    copies[1].wait()
     table[half:] = far[...].astype(jnp.float32)
+    copies[0].wait()
     pick_rows(rows, table, picked)
-    for copy in copies:
+    for copy in copies[2:]:
         copy.wait()
-    ones = jnp.ones((8, lanes), jnp.float32)
+    ones = jnp.ones((8, 3 * lanes), jnp.bfloat16)
     h_sum = jnp.zeros((rank, lanes), jnp.float32)
     d_sum = jnp.zeros((rank, lanes), jnp.float32)
     for k in range(half // CHUNK):
@@ -126,23 +138,23 @@
         scaled = upstream[here, :].astype(jnp.float32) * x
         x16 = x.astype(jnp.bfloat16)
         x_out[here, :] = x16
-        sums = dot_last(ones, scaled, lax.Precision.HIGHEST)
+        sums = dot_last(ones, jnp.concatenate(split3(scaled), axis=1))
         for j in range(CHUNK // 128):
             row = k * (CHUNK // 128) + j
-            bias_out[row : row + 1, :] = sums[:1, j * 128 : (j + 1) * 128]
+            part[2 * rank + row : 2 * rank + row + 1, :] = sums[:1, j * 128 : (j + 1) * 128]
         h_sum += jnp.dot(v_proj[:, here], x16, preferred_element_type=jnp.float32)
         d_sum += jnp.dot(
             u_proj[:, here], scaled.astype(jnp.bfloat16), preferred_element_type=jnp.float32
         )
     part[:rank] = h_sum
-    part[rank:] = d_sum
+    part[rank : 2 * rank] = d_sum
     part16[:rank] = h_sum.astype(jnp.bfloat16)
     part16[rank:] = d_sum.astype(jnp.bfloat16)
 
 
-def ranks_kernel(part, other, bias, ranks, message, total):
-    rows = part.shape[0]
-    value = part[...] + other[...].astype(jnp.float32)
+def ranks_kernel(part, other, ranks, message, total):
+    rows = other.shape[0]
+    value = part[:rows] + other[...].astype(jnp.float32)
     ranks[...] = value.astype(jnp.bfloat16)
     total[...] = value
     step = rows // 2 // 128
@@ -151,7 +163,7 @@
             to = i * rows // 2 + j * 128
             rank_rows = total[pl.ds(i * rows // 2 + j, 128, stride=step), :]
             message[to : to + 128, :] = rank_rows.astype(jnp.bfloat16)
-    store3(message, rows, bias[...])
+    store3(message, rows, part[rows:])
 
 
 def join_kernel(*rest):
@@ -274,31 +286,26 @@
     side = wire // block_rows % 2
     spot = wire // (2 * block_rows) * block_rows + wire % block_rows
     x_rows = jnp.where(side == t, 0, half_width) + spot
-    hbm = pltpu.with_memory_space_constraint
-    x_zero, part, part16, bias_part = local_call(
+    x_zero, part, part16 = local_call(
         forward_kernel,
         [
             array((half_width, samples), bf16),
-            array((2 * rank, samples), jnp.float32),
+            array((2 * rank + half_width // 128, samples), jnp.float32),
             array((2 * rank, samples), bf16),
-            array((half_width // 128, 128), jnp.float32),
-        ],
-        x_rows,
+        ],
         arrived,
-        partner,
-        upstream,
-        hbm(v_proj, pltpu.HBM),
-        hbm(u_proj, pltpu.HBM),
-        scalars=1,
+        *in_hbm(x_rows, partner, upstream, v_proj, u_proj),
         scratch_shapes=[
             pltpu.VMEM((2 * half_width, samples), jnp.float32),
             pltpu.VMEM((half_width, samples), jnp.float32),
+            pltpu.SMEM(x_rows.shape, jnp.int32),
+            pltpu.VMEM(partner.shape, bf16),
             pltpu.VMEM(upstream.shape, bf16),
             pltpu.VMEM(v_proj.shape, bf16),
             pltpu.VMEM(u_proj.shape, bf16),
-            pltpu.SemaphoreType.DMA((3,)),
-        ],
-        specs=[SMEM, VMEM, VMEM] + [pl.BlockSpec(memory_space=pltpu.HBM)] * 3,
+            pltpu.SemaphoreType.DMA((5,)),
+        ],
+        specs=[VMEM] + [HBM] * 5,
         mib=28,
     )
     other = lax.ppermute(part16, "t", SWAP)
@@ -310,7 +317,6 @@
         [array((2 * rank, samples), bf16), array((2 * rank + 128, samples), bf16)],
         part,
         other,
-        bias_part,
         scratch_shapes=[pltpu.VMEM((2 * rank, samples), jnp.float32)],
         mib=4,
     )

time: 195 us -> 196 us (level)
  transfers between devices with their start and end apart: 10 -> 10, of which waited for: 7 -> 7; matrix products, arithmetic and copies ran while one was open for 5% -> 6% of each run, Pallas kernels for 3% -> 3%
where the time goes in v3:
time: 196 us; the launch traced here: 192 us
  waiting for transfers between devices  67.1 us (34%)
  blocking collectives  58.2 us (30%)
  starting transfers between devices  30 us (15%)
  Pallas kernels  20.8 us (11%)
  matrix products  6.09 us (3%)
  local copies, waits for them, and re-layouts  4.74 us (2%)
  other arithmetic  4.6 us (2%)
    all_to_all x1, blocking collectives, step(): got = lax.all_to_all(outgoing, DP, split_axis=0, concat_axis=0, tiled=True)  58.2 us
    all_to_all x1, waiting for transfers between devices, step(): lax.all_to_all(looked, DP, split_axis=1, concat_axis=0, tiled=True)  29.2 us
    ppermute x1, waiting for transfers between devices, step(): partner = lax.ppermute(arrived, 't', SWAP)  19.6 us
    pallas_call x5, Pallas kernels, local_call(): pl.pallas_call(body, out_shape=out_shape, in_specs=specs or [SMEM] * scal...  15.3 us
    all_to_all x1, starting transfers between devices, step(): lax.all_to_all(looked, DP, split_axis=1, concat_axis=0, tiled=True)  14 us
    all_to_all x1, waiting for transfers between devices, step(): lax.all_to_all(x_zero.reshape(group, wide, samples), ('y', 'c'), split_ax...  8.03 us
    ppermute x3, waiting for transfers between devices, shift(): lax.ppermute(value, axis, [(i, (i + by) % size) for i in range(size)])  5.62 us
    pallas_call x1, Pallas kernels, gather(): pl.pallas_call(gather_kernel, out_shape=jax.ShapeDtypeStruct((dests, coun...  5.46 us
  transfers between devices with their start and end apart: 10, of which 7 were waited for; matrix products, arithmetic and copies ran while one was open for 6% of the time, Pallas kernels for 3%

profile of v3, /device:TPU:4, one launch (start us, length us, event | category | flops | bytes accessed | tf_op | source)
XLA Modules:
  0.0 192.4 jit_solution(12535120709722319249)
XLA Ops:
  0.7 1.2 copy-done
  1.9 1.1 copy_bitcast_fusion
  3.0 14.0 %all-to-all-start = ((bf16[32,128,128]{2,0,1:T(8,128)(2,1)}), bf16[32,128,128]{2,0,1:T(8,128)(2,1)S(1)}, u32[]{:S(2)}, u32[]{:S(2)}) async-start(bf16[32,128,128]{2,0,1:T(8,128)(2,1)} %copy_bitcast_fusion), calls=%async_computation | async-start | bytes 2097152 | tf_op jit(solution)/shard_map/all_to_all | solution.py:280
  17.1 29.2 %all-to-all-done = bf16[32,128,128]{2,0,1:T(8,128)(2,1)S(1)} async-done(((bf16[32,128,128]{2,0,1:T(8,128)(2,1)}), bf16[32,128,128]{2,0,1:T(8,128)(2,1)S(1)}, u32[]{:S(2)}, u32[]{:S(2)}) %all-to-all-start) | async-done | bytes 1048608 | tf_op jit(solution)/shard_map/all_to_all | solution.py:280
  47.1 3.8 %fusion.10 = (bf16[8192,128]{1,0:T(8,128)(2,1)S(1)}, bf16[8192,128]{1,0:T(8,128)(2,1)S(1)}) fusion(s32[8192]{0:T(1024)S(1)} %get-tuple-element.23, bf16[8192]{0:T(1024)(128)(2,1)S(1)} %get-tuple-element.26, bf16[8192]{0:T(1024)(128)(2,1)S(1)} %fusion.25), kind=kLoop, calls=%fused_computation.13 | loop fusion | flops 3145728 | bytes 4259840 | tf_op jit(solution)/shard_map/jit(_where)/select_n | solution.py:258
  52.3 19.6 %collective-permute-done.rest_1_ = bf16[4096,128]{1,0:T(8,128)(2,1)S(1)} collective-permute-done((bf16[4096,128]{1,0:T(8,128)(2,1)S(1)}, bf16[4096,128]{1,0:T(8,128)(2,1)S(1)}, u32[]{:S(2)}, u32[]{:S(2)}) %collective-permute-start) | collective-permute-done | bytes 1048608 | tf_op jit(solution)/shard_map/ppermute | solution.py:281
  72.0 1.0 copy-done.3
  72.9 7.7 %shard_map.93 = (bf16[4096,128]{1,0:T(8,128)(2,1)S(1)}, f32[800,128]{1,0:T(8,128)S(1)}, bf16[768,128]{1,0:T(8,128)(2,1)S(1)}) custom-call(bf16[4096,128]{1,0:T(8,128)(2,1)S(1)} %bitcast.30, s32[4096]{0:T(1024)} %fusion.36.rest_0_, bf16[4096,128]{1,0:T(8,128)(2,1)} %copy-done.3, bf16[4096,128]{1,0:T(8,128)(2,1)} %rest_2_.1, bf16[384,4096]{1,0:T(8,128)(2,1)} %rest_3_.1, ...), custom_call_target="tpu_custom_call" | custom-call | tf_op jit(solution)/shard_map/pallas_call | solution.py:60
  82.5 3.8 %all-to-all-start.2 = ((bf16[8,512,128]{2,1,0:T(8,128)(2,1)}), bf16[8,512,128]{2,1,0:T(8,128)(2,1)S(1)}, u32[]{:S(2)}, u32[]{:S(2)}) async-start(bf16[8,512,128]{2,1,0:T(8,128)(2,1)} %bitcast.32), calls=%async_computation.2 | async-start | bytes 2097152 | tf_op jit(solution)/shard_map/all_to_all | solution.py:282
  86.2 2.6 %collective-permute-done.1.other = bf16[768,128]{1,0:T(8,128)(2,1)S(1)} collective-permute-done((bf16[768,128]{1,0:T(8,128)(2,1)S(1)}, bf16[768,128]{1,0:T(8,128)(2,1)S(1)}, u32[]{:S(2)}, u32[]{:S(2)}) %collective-permute-start.1) | collective-permute-done | bytes 196640 | tf_op jit(solution)/shard_map/ppermute | solution.py:311
  88.9 1.1 collective-permute-start.3
  90.0 3.3 %collective-permute-start.4 = (bf16[896,128]{1,0:T(8,128)(2,1)S(1)}, bf16[896,128]{1,0:T(8,128)(2,1)}, u32[]{:S(2)}, u32[]{:S(2)}) collective-permute-start(bf16[896,128]{1,0:T(8,128)(2,1)S(1)} %get-tuple-element.17.rest_0_), channel_id=1, source_target_pairs={{0,8},{4,12},{8,0},{12,4},{1,9},{5,13},{9,1},{13,5},{2,10},{6,14},... | collective-permute-start | bytes 688136 | tf_op jit(solution)/shard_map/ppermute | solution.py:35
  93.8 3.8 %fusion.3 = f32[4096,128]{1,0:T(8,128)S(1)} fusion(bf16[384,4096]{1,0:T(8,128)(2,1)} %rest_4_.1, bf16[4096,128]{1,0:T(8,128)(2,1)} %rest_2_.1, f32[4096]{0:T(1024)S(1)} %copy-done.5, bf16[768,128]{1,0:T(8,128)(2,1)S(1)} %get-tuple-element.15), kind=kOutput, calls=%fused_computation.5 | convolution fusion | flops 404750336 | bytes 6406144 | tf_op jit(solution)/shard_map/dot_general | solution.py:29
  97.7 1.5 fusion.4.near
  99.2 1.6 collective-permute-start.2
  100.7 2.1 %all-to-all-done.2.up_group = bf16[8,512,128]{2,1,0:T(8,128)(2,1)S(1)} async-done(((bf16[8,512,128]{2,1,0:T(8,128)(2,1)}), bf16[8,512,128]{2,1,0:T(8,128)(2,1)S(1)}, u32[]{:S(2)}, u32[]{:S(2)}) %all-to-all-start.2) | async-done | bytes 1048608 | tf_op jit(solution)/shard_map/all_to_all | solution.py:282
  102.8 4.2 %all-to-all-start.1 = ((bf16[8,512,128]{2,1,0:T(8,128)(2,1)}), bf16[8,512,128]{2,1,0:T(8,128)(2,1)}, u32[]{:S(2)}, u32[]{:S(2)}) async-start(bf16[8,512,128]{2,1,0:T(8,128)(2,1)} %bitcast.31), calls=%async_computation.1 | async-start | bytes 2097152 | tf_op jit(solution)/shard_map/all_to_all | solution.py:312
  107.1 5.5 %collective-permute-done.4.rest_2_ = bf16[896,128]{1,0:T(8,128)(2,1)} collective-permute-done((bf16[896,128]{1,0:T(8,128)(2,1)S(1)}, bf16[896,128]{1,0:T(8,128)(2,1)}, u32[]{:S(2)}, u32[]{:S(2)}) %collective-permute-start.4) | collective-permute-done | bytes 229408 | tf_op jit(solution)/shard_map/ppermute | solution.py:35
  112.7 2.1 %shard_map.95.near_ranks = bf16[3200,128]{1,0:T(8,128)(2,1)} custom-call(bf16[896,128]{1,0:T(8,128)(2,1)S(1)} %get-tuple-element.17.rest_0_, bf16[896,128]{1,0:T(8,128)(2,1)} %collective-permute-done.3.rest_1_, bf16[896,128]{1,0:T(8,128)(2,1)} %collective-permute-done.4.rest_2_, bf16[896,128]{1,0:T(8,128)(2,1)} %collective-permute-done.5.rest_3_), custom_call_target="tpu_custom_call" | custom-call | tf_op jit(solution)/shard_map/pallas_call | solution.py:60
  115.3 8.0 %all-to-all-done.1.x_group = bf16[8,512,128]{2,1,0:T(8,128)(2,1)} async-done(((bf16[8,512,128]{2,1,0:T(8,128)(2,1)}), bf16[8,512,128]{2,1,0:T(8,128)(2,1)}, u32[]{:S(2)}, u32[]{:S(2)}) %all-to-all-start.1) | async-done | bytes 1048608 | tf_op jit(solution)/shard_map/all_to_all | solution.py:312
  123.4 4.1 %shard_map.96.extra = bf16[128,32,128]{2,1,0:T(8,128)(2,1)S(1)} custom-call(s32[2]{0:T(128)S(1)} %pad_add_fusion.place, bf16[8,512,128]{2,1,0:T(8,128)(2,1)} %all-to-all-done.1.x_group, bf16[8,512,128]{2,1,0:T(8,128)(2,1)S(1)} %all-to-all-done.2.up_group, bf16[3200,128]{1,0:T(8,128)(2,1)} %shard_map.95.near_ranks, ...), custom_call_target="tpu_custom_call" | custom-call | tf_op jit(solution)/shard_map/pallas_call | solution.py:60
  127.5 5.5 %gather_rows.1 = bf16[128,64,128]{2,1,0:T(8,128)(2,1)S(1)} custom-call(s32[4096]{0:T(1024)S(1)} %fusion.30.rows, bf16[4096,128]{1,0:T(8,128)(2,1)S(1)} %fusion.4.near, bf16[4096,128]{1,0:T(8,128)(2,1)} %collective-permute-done.2.far, bf16[128,32,128]{2,1,0:T(8,128)(2,1)S(1)} %shard_map.96.extra), custom_call_target="tpu_custom_call" | custom-call | tf_op jit(solution)/shard_map/gather_rows/pallas_call | solution.py:94
  132.9 58.2 %all_to_all.34.refs_0_ = bf16[128,64,128]{2,1,0:T(8,128)(2,1)S(1)} all-to-all(bf16[128,64,128]{2,1,0:T(8,128)(2,1)S(1)} %gather_rows.1), channel_id=1, replica_groups=mesh['z'=8,'xl'=2,'y'=4,'c'=2,'t'=2] {'z','xl','y','c'}, dimensions={0} | all-to-all | bytes 4194304 | tf_op jit(solution)/shard_map/all_to_all | solution.py:357
  191.1 1.3 shard_map.97
  (28 shorter events, 5.3 us)
Async XLA Ops:
  0.6 1.2 copy-start
  0.6 16.4 %copy-start.4 = (s32[8192]{0:T(1024)S(1)}, s32[8192]{0:T(1024)}, u32[]{:S(2)}) copy-start(s32[8192]{0:T(1024)} %param.7) | copy-start | bytes 98308
  3.0 43.2 %all-to-all-start = ((bf16[32,128,128]{2,0,1:T(8,128)(2,1)}), bf16[32,128,128]{2,0,1:T(8,128)(2,1)S(1)}, u32[]{:S(2)}, u32[]{:S(2)}) async-start(bf16[32,128,128]{2,0,1:T(8,128)(2,1)} %copy_bitcast_fusion), calls=%async_computation | async-start | bytes 2097152 | tf_op jit(solution)/shard_map/all_to_all | solution.py:280
  46.3 25.7 %collective-permute-start = (bf16[4096,128]{1,0:T(8,128)(2,1)S(1)}, bf16[4096,128]{1,0:T(8,128)(2,1)S(1)}, u32[]{:S(2)}, u32[]{:S(2)}) collective-permute-start(bf16[4096,128]{1,0:T(8,128)(2,1)S(1)} %bitcast.29), channel_id=1, source_target_pairs={{0,1},{1,0},{2,3},{3,2},{4,5},{5,4},{6,7},{7,6},{8,9},{9,8},{10,11... | collective-permute-start | bytes 3145736 | tf_op jit(solution)/shard_map/ppermute | solution.py:281
  72.0 1.0 copy-start.3
  80.7 1.0 copy-start.1
  81.6 12.2 %copy-start.5 = (f32[4096]{0:T(1024)S(1)}, f32[4096]{0:T(1024)}, u32[]{:S(2)}) copy-start(f32[4096]{0:T(1024)} %param.10) | copy-start | bytes 49156
  81.7 7.2 %collective-permute-start.1 = (bf16[768,128]{1,0:T(8,128)(2,1)S(1)}, bf16[768,128]{1,0:T(8,128)(2,1)S(1)}, u32[]{:S(2)}, u32[]{:S(2)}) collective-permute-start(bf16[768,128]{1,0:T(8,128)(2,1)S(1)} %get-tuple-element.14), channel_id=1, source_target_pairs={{0,1},{1,0},{2,3},{3,2},{4,5},{5,4},{6,7},{7,6},{8,9},{9,8},{10,11... | collective-permute-start | bytes 589832 | tf_op jit(solution)/shard_map/ppermute | solution.py:311
  82.5 20.3 %all-to-all-start.2 = ((bf16[8,512,128]{2,1,0:T(8,128)(2,1)}), bf16[8,512,128]{2,1,0:T(8,128)(2,1)S(1)}, u32[]{:S(2)}, u32[]{:S(2)}) async-start(bf16[8,512,128]{2,1,0:T(8,128)(2,1)} %bitcast.32), calls=%async_computation.2 | async-start | bytes 2097152 | tf_op jit(solution)/shard_map/all_to_all | solution.py:282
  88.9 18.2 %collective-permute-start.3 = (bf16[896,128]{1,0:T(8,128)(2,1)S(1)}, bf16[896,128]{1,0:T(8,128)(2,1)}, u32[]{:S(2)}, u32[]{:S(2)}) collective-permute-start(bf16[896,128]{1,0:T(8,128)(2,1)S(1)} %get-tuple-element.17.rest_0_), channel_id=1, source_target_pairs={{0,4},{4,8},{8,12},{12,0},{1,5},{5,9},{9,13},{13,1},{2,6},{6,10},{... | collective-permute-start | bytes 688136 | tf_op jit(solution)/shard_map/ppermute | solution.py:35
  90.0 22.7 %collective-permute-start.4 = (bf16[896,128]{1,0:T(8,128)(2,1)S(1)}, bf16[896,128]{1,0:T(8,128)(2,1)}, u32[]{:S(2)}, u32[]{:S(2)}) collective-permute-start(bf16[896,128]{1,0:T(8,128)(2,1)S(1)} %get-tuple-element.17.rest_0_), channel_id=1, source_target_pairs={{0,8},{4,12},{8,0},{12,4},{1,9},{5,13},{9,1},{13,5},{2,10},{6,14},... | collective-permute-start | bytes 688136 | tf_op jit(solution)/shard_map/ppermute | solution.py:35
  93.3 19.3 %collective-permute-start.5 = (bf16[896,128]{1,0:T(8,128)(2,1)S(1)}, bf16[896,128]{1,0:T(8,128)(2,1)}, u32[]{:S(2)}, u32[]{:S(2)}) collective-permute-start(bf16[896,128]{1,0:T(8,128)(2,1)S(1)} %get-tuple-element.17.rest_0_), channel_id=1, source_target_pairs={{0,12},{4,0},{8,4},{12,8},{1,13},{5,1},{9,5},{13,9},{2,14},{6,2},{... | collective-permute-start | bytes 688136 | tf_op jit(solution)/shard_map/ppermute | solution.py:35
  93.8 3.8 %copy-start.2 = (bf16[384,4096]{1,0:T(8,128)(2,1)S(1)}, bf16[384,4096]{1,0:T(8,128)(2,1)}, u32[]{:S(2)}) copy-start(bf16[384,4096]{1,0:T(8,128)(2,1)} %rest_3_.1) | copy-start | bytes 9437188
  99.2 28.3 %collective-permute-start.2 = (bf16[4096,128]{1,0:T(8,128)(2,1)S(1)}, bf16[4096,128]{1,0:T(8,128)(2,1)}, u32[]{:S(2)}, u32[]{:S(2)}) collective-permute-start(bf16[4096,128]{1,0:T(8,128)(2,1)S(1)} %fusion.4.near), channel_id=1, source_target_pairs={{0,1},{1,0},{2,3},{3,2},{4,5},{5,4},{6,7},{7,6},{8,9},{9,8},{10,11... | collective-permute-start | bytes 3145736 | tf_op jit(solution)/shard_map/ppermute | solution.py:327
  102.8 20.6 %all-to-all-start.1 = ((bf16[8,512,128]{2,1,0:T(8,128)(2,1)}), bf16[8,512,128]{2,1,0:T(8,128)(2,1)}, u32[]{:S(2)}, u32[]{:S(2)}) async-start(bf16[8,512,128]{2,1,0:T(8,128)(2,1)} %bitcast.31), calls=%async_computation.1 | async-start | bytes 2097152 | tf_op jit(solution)/shard_map/all_to_all | solution.py:312
  114.8 8.6 %collective-permute-start.6 = (bf16[3200,128]{1,0:T(8,128)(2,1)}, bf16[3200,128]{1,0:T(8,128)(2,1)}, u32[]{:S(2)}, u32[]{:S(2)}) collective-permute-start(bf16[3200,128]{1,0:T(8,128)(2,1)} %shard_map.95.near_ranks), channel_id=1, source_target_pairs={{0,2},{2,0},{1,3},{3,1},{4,6},{6,4},{5,7},{7,5},{8,10},{10,8},{9,1... | collective-permute-start | bytes 2457608 | tf_op jit(solution)/shard_map/ppermute | solution.py:333

commit v4 on v3

--- a/solution.py
+++ b/solution.py
@@ -56,12 +56,12 @@
     out[start + 3 * rows : start + 4 * rows, :] = jnp.zeros((rows, value.shape[1]), jnp.bfloat16)
 
 
-def local_call(body, out_shape, *args, scalars=0, mib, specs=None, **kwargs):
+def local_call(body, out_shape, *args, scalars=0, mib, specs=None, outs=None, **kwargs):
     return pl.pallas_call(
         body,
         out_shape=out_shape,
         in_specs=specs or [SMEM] * scalars + [VMEM] * (len(args) - scalars),
-        out_specs=jax.tree.map(lambda _: VMEM, out_shape),
+        out_specs=outs or jax.tree.map(lambda _: VMEM, out_shape),
         compiler_params=pltpu.CompilerParams(vmem_limit_bytes=mib * 2**20),
         **kwargs,
     )(*args)
@@ -77,28 +77,35 @@
     lax.fori_loop(0, picked.shape[0] // UNROLL, step, 0)
 
 
-def gather_kernel(rows, near, far, extra, out, table, picked):
+def gather_kernel(rows_in, near, far_in, extra, out, rows, far, table, picked, sems):
     half = near.shape[0]
     dests, height, lanes = out.shape
     block = height - extra.shape[1]
+    copies = start_copies(((far_in, far), (rows_in, rows), (extra, out.at[:, block:, :])), sems)
     table[:half] = near[...].astype(jnp.float32)
+    copies[0].wait()
     table[half:] = far[...].astype(jnp.float32)
+    copies[1].wait()
     pick_rows(rows, table, picked)
     out[:, :block, :] = picked[...].reshape(dests, block, lanes).astype(out.dtype)
-    out[:, block:, :] = extra[...]
+    copies[2].wait()
 
 
 def gather(rows, near, far, extra):
     count, lanes = rows.shape[0], near.shape[1]
     dests, height, _ = extra.shape
+    rows, far = in_hbm(rows, far)
     return pl.pallas_call(
         gather_kernel,
         out_shape=jax.ShapeDtypeStruct((dests, count // dests + height, lanes), near.dtype),
-        in_specs=[SMEM, VMEM, VMEM, VMEM],
+        in_specs=[HBM, VMEM, HBM, VMEM],
         out_specs=VMEM,
         scratch_shapes=[
+            pltpu.SMEM((count,), jnp.int32),
+            pltpu.VMEM(near.shape, near.dtype),
             pltpu.VMEM((2 * near.shape[0], lanes), jnp.float32),
             pltpu.VMEM((count, lanes), jnp.float32),
+            pltpu.SemaphoreType.DMA((3,)),
         ],
         compiler_params=pltpu.CompilerParams(vmem_limit_bytes=16 * 2**20),
         name="gather_rows",
@@ -119,7 +126,8 @@
 def forward_kernel(near, *rest):
     sources, (x_out, part, part16, table, picked, *copied, sems) = rest[:5], rest[5:]
     copies = start_copies(zip(sources, copied), sems)
-    rows, far, upstream, v_proj, u_proj = copied
+    rows, far, upstream, v_proj, u_proj, staged = copied
+    sent = []
     half, lanes = near.shape
     rank = v_proj.shape[0]
     table[:half] = near[...].astype(jnp.float32)
@@ -137,7 +145,9 @@
         x = picked[here, :]
         scaled = upstream[here, :].astype(jnp.float32) * x
         x16 = x.astype(jnp.bfloat16)
-        x_out[here, :] = x16
+        staged[here, :] = x16
+        sent.append(pltpu.make_async_copy(staged.at[here], x_out.at[here], sems.at[5 + k]))
+        sent[-1].start()
         sums = dot_last(ones, jnp.concatenate(split3(scaled), axis=1))
         for j in range(CHUNK // 128):
             row = k * (CHUNK // 128) + j
@@ -150,6 +160,8 @@
     part[rank : 2 * rank] = d_sum
     part16[:rank] = h_sum.astype(jnp.bfloat16)
     part16[rank:] = d_sum.astype(jnp.bfloat16)
+    for copy in sent:
+        copy.wait()
 
 
 def ranks_kernel(part, other, ranks, message, total):
@@ -303,9 +315,12 @@
             pltpu.VMEM(upstream.shape, bf16),
             pltpu.VMEM(v_proj.shape, bf16),
             pltpu.VMEM(u_proj.shape, bf16),
-            pltpu.SemaphoreType.DMA((5,)),
+            pltpu.VMEM(upstream.shape, bf16),
+            pltpu.SemaphoreType.DMA((5 + half_width // CHUNK,)),
         ],
         specs=[VMEM] + [HBM] * 5,
+        outs=[HBM, VMEM, VMEM],
+        input_output_aliases={2: 0},
         mib=28,
     )
     other = lax.ppermute(part16, "t", SWAP)

time: 196 us -> 196 us (level)
  Pallas kernels: 20.8 us -> 22.8 us
    pallas_call x5, Pallas kernels: 15.3 us -> 17.6 us  [local_call(): pl.pallas_call(body, out_shape=out_shape, in_specs=specs or [SMEM] * scal...]
  transfers between devices with their start and end apart: 10 -> 10, of which waited for: 7 -> 6; matrix products, arithmetic and copies ran while one was open for 6% -> 6% of each run, Pallas kernels for 3% -> 4%
where the time goes in v4:
time: 196 us; the launch traced here: 193 us
  waiting for transfers between devices  66.1 us (34%)
  blocking collectives  58.2 us (30%)
  starting transfers between devices  29.8 us (15%)
  Pallas kernels  22.8 us (12%)
  matrix products  6.09 us (3%)
  other arithmetic  5.2 us (3%)
  local copies, waits for them, and re-layouts  3.78 us (2%)
    all_to_all x1, blocking collectives, step(): got = lax.all_to_all(outgoing, DP, split_axis=0, concat_axis=0, tiled=True)  58.2 us
    all_to_all x1, waiting for transfers between devices, step(): lax.all_to_all(looked, DP, split_axis=1, concat_axis=0, tiled=True)  29.2 us
    ppermute x1, waiting for transfers between devices, step(): partner = lax.ppermute(arrived, 't', SWAP)  19.6 us
    pallas_call x5, Pallas kernels, local_call(): pl.pallas_call(body, out_shape=out_shape, in_specs=specs or [SMEM] * scal...  17.6 us
    all_to_all x1, starting transfers between devices, step(): lax.all_to_all(looked, DP, split_axis=1, concat_axis=0, tiled=True)  14 us
    all_to_all x1, waiting for transfers between devices, step(): lax.all_to_all(x_zero.reshape(group, wide, samples), ('y', 'c'), split_ax...  7.43 us
    ppermute x3, waiting for transfers between devices, shift(): lax.ppermute(value, axis, [(i, (i + by) % size) for i in range(size)])  5.61 us
    dot_general x2, matrix products, dot_first(): lax.dot_general(left, right, (((0,), (0,)), ((), ())), preferred_element_...  5.29 us
  transfers between devices with their start and end apart: 10, of which 6 were waited for; matrix products, arithmetic and copies ran while one was open for 6% of the time, Pallas kernels for 4%

profile of v4, /device:TPU:4, one launch (start us, length us, event | category | flops | bytes accessed | tf_op | source)
XLA Modules:
  0.0 192.9 jit_solution(4705127969481216917)
XLA Ops:
  0.7 1.2 copy-done
  1.9 1.1 copy_bitcast_fusion
  3.0 14.0 %all-to-all-start = ((bf16[32,128,128]{2,0,1:T(8,128)(2,1)}), bf16[32,128,128]{2,0,1:T(8,128)(2,1)S(1)}, u32[]{:S(2)}, u32[]{:S(2)}) async-start(bf16[32,128,128]{2,0,1:T(8,128)(2,1)} %copy_bitcast_fusion), calls=%async_computation | async-start | bytes 2097152 | tf_op jit(solution)/shard_map/all_to_all | solution.py:292
  17.1 29.2 %all-to-all-done = bf16[32,128,128]{2,0,1:T(8,128)(2,1)S(1)} async-done(((bf16[32,128,128]{2,0,1:T(8,128)(2,1)}), bf16[32,128,128]{2,0,1:T(8,128)(2,1)S(1)}, u32[]{:S(2)}, u32[]{:S(2)}) %all-to-all-start) | async-done | bytes 1048608 | tf_op jit(solution)/shard_map/all_to_all | solution.py:292
  47.1 3.8 %fusion.10 = (bf16[8192,128]{1,0:T(8,128)(2,1)S(1)}, bf16[8192,128]{1,0:T(8,128)(2,1)S(1)}) fusion(s32[8192]{0:T(1024)S(1)} %get-tuple-element.23, bf16[8192]{0:T(1024)(128)(2,1)S(1)} %get-tuple-element.26, bf16[8192]{0:T(1024)(128)(2,1)S(1)} %fusion.25), kind=kLoop, calls=%fused_computation.13 | loop fusion | flops 3145728 | bytes 4259840 | tf_op jit(solution)/shard_map/jit(_where)/select_n | solution.py:270
  52.3 19.6 %collective-permute-done.rest_1_ = bf16[4096,128]{1,0:T(8,128)(2,1)S(1)} collective-permute-done((bf16[4096,128]{1,0:T(8,128)(2,1)S(1)}, bf16[4096,128]{1,0:T(8,128)(2,1)S(1)}, u32[]{:S(2)}, u32[]{:S(2)}) %collective-permute-start) | collective-permute-done | bytes 1048608 | tf_op jit(solution)/shard_map/ppermute | solution.py:293
  72.0 1.0 copy-done.2
  72.9 9.3 %shard_map.93 = (bf16[4096,128]{1,0:T(8,128)(2,1)}, f32[800,128]{1,0:T(8,128)S(1)}, bf16[768,128]{1,0:T(8,128)(2,1)}) custom-call(bf16[4096,128]{1,0:T(8,128)(2,1)S(1)} %bitcast.30, s32[4096]{0:T(1024)} %fusion.36.rest_0_, bf16[4096,128]{1,0:T(8,128)(2,1)} %copy-done.2, bf16[4096,128]{1,0:T(8,128)(2,1)} %rest_2_.1, ...), custom_call_target="tpu_custom_call", output_to_operand_aliasing={{0}: (2, {})} | custom-call | tf_op jit(solution)/shard_map/pallas_call | solution.py:60
  83.2 3.8 %all-to-all-start.2 = ((bf16[8,512,128]{2,1,0:T(8,128)(2,1)}), bf16[8,512,128]{2,1,0:T(8,128)(2,1)S(1)}, u32[]{:S(2)}, u32[]{:S(2)}) async-start(bf16[8,512,128]{2,1,0:T(8,128)(2,1)} %bitcast.31), calls=%async_computation.2 | async-start | bytes 2097152 | tf_op jit(solution)/shard_map/all_to_all | solution.py:294
  86.9 2.8 %collective-permute-done.1.other = bf16[768,128]{1,0:T(8,128)(2,1)S(1)} collective-permute-done((bf16[768,128]{1,0:T(8,128)(2,1)}, bf16[768,128]{1,0:T(8,128)(2,1)S(1)}, u32[]{:S(2)}, u32[]{:S(2)}) %collective-permute-start.1) | collective-permute-done | bytes 196640 | tf_op jit(solution)/shard_map/ppermute | solution.py:326
  90.5 1.0 collective-permute-start.3
  91.5 3.3 %collective-permute-start.4 = (bf16[896,128]{1,0:T(8,128)(2,1)}, bf16[896,128]{1,0:T(8,128)(2,1)}, u32[]{:S(2)}, u32[]{:S(2)}) collective-permute-start(bf16[896,128]{1,0:T(8,128)(2,1)} %get-tuple-element.17.rest_0_), channel_id=1, source_target_pairs={{0,8},{4,12},{8,0},{12,4},{1,9},{5,13},{9,1},{13,5},{2,10},{6,14},... | collective-permute-start | bytes 688136 | tf_op jit(solution)/shard_map/ppermute | solution.py:35
  95.4 3.8 %fusion.3 = f32[4096,128]{1,0:T(8,128)S(1)} fusion(bf16[384,4096]{1,0:T(8,128)(2,1)} %rest_4_.1, bf16[4096,128]{1,0:T(8,128)(2,1)} %rest_2_.1, f32[4096]{0:T(1024)S(1)} %copy-done.4, bf16[768,128]{1,0:T(8,128)(2,1)S(1)} %get-tuple-element.15), kind=kOutput, calls=%fused_computation.5 | convolution fusion | flops 404750336 | bytes 6406144 | tf_op jit(solution)/shard_map/dot_general | solution.py:29
  99.2 1.5 fusion.4.near
  100.7 1.3 collective-permute-start.2
  102.0 1.5 all-to-all-done.2.up_group
  103.5 4.2 %all-to-all-start.1 = ((bf16[8,512,128]{2,1,0:T(8,128)(2,1)}), bf16[8,512,128]{2,1,0:T(8,128)(2,1)}, u32[]{:S(2)}, u32[]{:S(2)}) async-start(bf16[8,512,128]{2,1,0:T(8,128)(2,1)} %bitcast.32), calls=%async_computation.1 | async-start | bytes 2097152 | tf_op jit(solution)/shard_map/all_to_all | solution.py:327
  107.7 5.6 %collective-permute-done.4.rest_2_ = bf16[896,128]{1,0:T(8,128)(2,1)} collective-permute-done((bf16[896,128]{1,0:T(8,128)(2,1)}, bf16[896,128]{1,0:T(8,128)(2,1)}, u32[]{:S(2)}, u32[]{:S(2)}) %collective-permute-start.4) | collective-permute-done | bytes 229408 | tf_op jit(solution)/shard_map/ppermute | solution.py:35
  113.3 2.1 %shard_map.95.near_ranks = bf16[3200,128]{1,0:T(8,128)(2,1)} custom-call(bf16[896,128]{1,0:T(8,128)(2,1)} %get-tuple-element.17.rest_0_, bf16[896,128]{1,0:T(8,128)(2,1)S(1)} %collective-permute-done.3.rest_1_, bf16[896,128]{1,0:T(8,128)(2,1)} %collective-permute-done.4.rest_2_, bf16[896,128]{1,0:T(8,128)(2,1)} %collective-permute-done.5.rest_3_), custom_call_target="tpu_custom_call" | custom-call | tf_op jit(solution)/shard_map/pallas_call | solution.py:60
  116.7 7.4 %all-to-all-done.1.x_group = bf16[8,512,128]{2,1,0:T(8,128)(2,1)} async-done(((bf16[8,512,128]{2,1,0:T(8,128)(2,1)}), bf16[8,512,128]{2,1,0:T(8,128)(2,1)}, u32[]{:S(2)}, u32[]{:S(2)}) %all-to-all-start.1) | async-done | bytes 1048608 | tf_op jit(solution)/shard_map/all_to_all | solution.py:327
  124.1 4.1 %shard_map.96.extra = bf16[128,32,128]{2,1,0:T(8,128)(2,1)S(1)} custom-call(s32[2]{0:T(128)S(1)} %pad_add_fusion.place, bf16[8,512,128]{2,1,0:T(8,128)(2,1)} %all-to-all-done.1.x_group, bf16[8,512,128]{2,1,0:T(8,128)(2,1)S(1)} %all-to-all-done.2.up_group, bf16[3200,128]{1,0:T(8,128)(2,1)} %shard_map.95.near_ranks, ...), custom_call_target="tpu_custom_call" | custom-call | tf_op jit(solution)/shard_map/pallas_call | solution.py:60
  128.2 5.3 %gather_rows.1 = bf16[128,64,128]{2,1,0:T(8,128)(2,1)S(1)} custom-call(s32[4096]{0:T(1024)} %fusion.30.rows_in, bf16[4096,128]{1,0:T(8,128)(2,1)S(1)} %fusion.4.near, bf16[4096,128]{1,0:T(8,128)(2,1)} %collective-permute-done.2.far_in, bf16[128,32,128]{2,1,0:T(8,128)(2,1)S(1)} %shard_map.96.extra), custom_call_target="tpu_custom_call" | custom-call | tf_op jit(solution)/shard_map/gather_rows/pallas_call | solution.py:98
  133.4 58.2 %all_to_all.34.refs_0_ = bf16[128,64,128]{2,1,0:T(8,128)(2,1)S(1)} all-to-all(bf16[128,64,128]{2,1,0:T(8,128)(2,1)S(1)} %gather_rows.1), channel_id=1, replica_groups=mesh['z'=8,'xl'=2,'y'=4,'c'=2,'t'=2] {'z','xl','y','c'}, dimensions={0} | all-to-all | bytes 4194304 | tf_op jit(solution)/shard_map/all_to_all | solution.py:372
  191.6 1.3 shard_map.97
  (26 shorter events, 5.7 us)
Async XLA Ops:
  0.6 1.2 copy-start
  0.6 16.4 %copy-start.3 = (s32[8192]{0:T(1024)S(1)}, s32[8192]{0:T(1024)}, u32[]{:S(2)}) copy-start(s32[8192]{0:T(1024)} %param.7) | copy-start | bytes 98308
  3.0 43.2 %all-to-all-start = ((bf16[32,128,128]{2,0,1:T(8,128)(2,1)}), bf16[32,128,128]{2,0,1:T(8,128)(2,1)S(1)}, u32[]{:S(2)}, u32[]{:S(2)}) async-start(bf16[32,128,128]{2,0,1:T(8,128)(2,1)} %copy_bitcast_fusion), calls=%async_computation | async-start | bytes 2097152 | tf_op jit(solution)/shard_map/all_to_all | solution.py:292
  46.3 25.7 %collective-permute-start = (bf16[4096,128]{1,0:T(8,128)(2,1)S(1)}, bf16[4096,128]{1,0:T(8,128)(2,1)S(1)}, u32[]{:S(2)}, u32[]{:S(2)}) collective-permute-start(bf16[4096,128]{1,0:T(8,128)(2,1)S(1)} %bitcast.29), channel_id=1, source_target_pairs={{0,1},{1,0},{2,3},{3,2},{4,5},{5,4},{6,7},{7,6},{8,9},{9,8},{10,11... | collective-permute-start | bytes 3145736 | tf_op jit(solution)/shard_map/ppermute | solution.py:293
  72.0 1.0 copy-start.2
  82.3 13.1 %copy-start.4 = (f32[4096]{0:T(1024)S(1)}, f32[4096]{0:T(1024)}, u32[]{:S(2)}) copy-start(f32[4096]{0:T(1024)} %param.10) | copy-start | bytes 49156
  82.3 7.5 %collective-permute-start.1 = (bf16[768,128]{1,0:T(8,128)(2,1)}, bf16[768,128]{1,0:T(8,128)(2,1)S(1)}, u32[]{:S(2)}, u32[]{:S(2)}) collective-permute-start(bf16[768,128]{1,0:T(8,128)(2,1)} %get-tuple-element.14), channel_id=1, source_target_pairs={{0,1},{1,0},{2,3},{3,2},{4,5},{5,4},{6,7},{7,6},{8,9},{9,8},{10,11... | collective-permute-start | bytes 589832 | tf_op jit(solution)/shard_map/ppermute | solution.py:326
  83.2 20.3 %all-to-all-start.2 = ((bf16[8,512,128]{2,1,0:T(8,128)(2,1)}), bf16[8,512,128]{2,1,0:T(8,128)(2,1)S(1)}, u32[]{:S(2)}, u32[]{:S(2)}) async-start(bf16[8,512,128]{2,1,0:T(8,128)(2,1)} %bitcast.31), calls=%async_computation.2 | async-start | bytes 2097152 | tf_op jit(solution)/shard_map/all_to_all | solution.py:294
  90.5 17.2 %collective-permute-start.3 = (bf16[896,128]{1,0:T(8,128)(2,1)}, bf16[896,128]{1,0:T(8,128)(2,1)S(1)}, u32[]{:S(2)}, u32[]{:S(2)}) collective-permute-start(bf16[896,128]{1,0:T(8,128)(2,1)} %get-tuple-element.17.rest_0_), channel_id=1, source_target_pairs={{0,4},{4,8},{8,12},{12,0},{1,5},{5,9},{9,13},{13,1},{2,6},{6,10},{... | collective-permute-start | bytes 688136 | tf_op jit(solution)/shard_map/ppermute | solution.py:35
  91.5 21.8 %collective-permute-start.4 = (bf16[896,128]{1,0:T(8,128)(2,1)}, bf16[896,128]{1,0:T(8,128)(2,1)}, u32[]{:S(2)}, u32[]{:S(2)}) collective-permute-start(bf16[896,128]{1,0:T(8,128)(2,1)} %get-tuple-element.17.rest_0_), channel_id=1, source_target_pairs={{0,8},{4,12},{8,0},{12,4},{1,9},{5,13},{9,1},{13,5},{2,10},{6,14},... | collective-permute-start | bytes 688136 | tf_op jit(solution)/shard_map/ppermute | solution.py:35
  94.8 18.5 %collective-permute-start.5 = (bf16[896,128]{1,0:T(8,128)(2,1)}, bf16[896,128]{1,0:T(8,128)(2,1)}, u32[]{:S(2)}, u32[]{:S(2)}) collective-permute-start(bf16[896,128]{1,0:T(8,128)(2,1)} %get-tuple-element.17.rest_0_), channel_id=1, source_target_pairs={{0,12},{4,0},{8,4},{12,8},{1,13},{5,1},{9,5},{13,9},{2,14},{6,2},{... | collective-permute-start | bytes 688136 | tf_op jit(solution)/shard_map/ppermute | solution.py:35
  95.4 3.8 %copy-start.1 = (bf16[384,4096]{1,0:T(8,128)(2,1)S(1)}, bf16[384,4096]{1,0:T(8,128)(2,1)}, u32[]{:S(2)}) copy-start(bf16[384,4096]{1,0:T(8,128)(2,1)} %rest_3_.1) | copy-start | bytes 9437188
  100.7 27.5 %collective-permute-start.2 = (bf16[4096,128]{1,0:T(8,128)(2,1)S(1)}, bf16[4096,128]{1,0:T(8,128)(2,1)}, u32[]{:S(2)}, u32[]{:S(2)}) collective-permute-start(bf16[4096,128]{1,0:T(8,128)(2,1)S(1)} %fusion.4.near), channel_id=1, source_target_pairs={{0,1},{1,0},{2,3},{3,2},{4,5},{5,4},{6,7},{7,6},{8,9},{9,8},{10,11... | collective-permute-start | bytes 3145736 | tf_op jit(solution)/shard_map/ppermute | solution.py:342
  103.5 20.6 %all-to-all-start.1 = ((bf16[8,512,128]{2,1,0:T(8,128)(2,1)}), bf16[8,512,128]{2,1,0:T(8,128)(2,1)}, u32[]{:S(2)}, u32[]{:S(2)}) async-start(bf16[8,512,128]{2,1,0:T(8,128)(2,1)} %bitcast.32), calls=%async_computation.1 | async-start | bytes 2097152 | tf_op jit(solution)/shard_map/all_to_all | solution.py:327
  115.5 8.6 %collective-permute-start.6 = (bf16[3200,128]{1,0:T(8,128)(2,1)}, bf16[3200,128]{1,0:T(8,128)(2,1)}, u32[]{:S(2)}, u32[]{:S(2)}) collective-permute-start(bf16[3200,128]{1,0:T(8,128)(2,1)} %shard_map.95.near_ranks), channel_id=1, source_target_pairs={{0,2},{2,0},{1,3},{3,1},{4,6},{6,4},{5,7},{7,5},{8,10},{10,8},{9,1... | collective-permute-start | bytes 2457608 | tf_op jit(solution)/shard_map/ppermute | solution.py:348

commit v5 on v4

--- a/solution.py
+++ b/solution.py
@@ -41,19 +41,6 @@
     middle = rest.astype(jnp.bfloat16)
     low = (rest - middle.astype(jnp.float32)).astype(jnp.bfloat16)
     return high, middle, low
-
-
-def join3(parts):
-    rows = parts.shape[0] // 4
-    wide = parts.astype(jnp.float32)
-    return wide[:rows] + wide[rows : 2 * rows] + wide[2 * rows : 3 * rows]
-
-
-def store3(out, start, value):
-    rows = value.shape[0]
-    for i, part in enumerate(split3(value)):
-        out[start + i * rows : start + (i + 1) * rows, :] = part
-    out[start + 3 * rows : start + 4 * rows, :] = jnp.zeros((rows, value.shape[1]), jnp.bfloat16)
 
 
 def local_call(body, out_shape, *args, scalars=0, mib, specs=None, outs=None, **kwargs):
@@ -137,7 +124,6 @@
     pick_rows(rows, table, picked)
     for copy in copies[2:]:
         copy.wait()
-    ones = jnp.ones((8, 3 * lanes), jnp.bfloat16)
     h_sum = jnp.zeros((rank, lanes), jnp.float32)
     d_sum = jnp.zeros((rank, lanes), jnp.float32)
     for k in range(half // CHUNK):
@@ -148,16 +134,12 @@
         staged[here, :] = x16
         sent.append(pltpu.make_async_copy(staged.at[here], x_out.at[here], sems.at[5 + k]))
         sent[-1].start()
-        sums = dot_last(ones, jnp.concatenate(split3(scaled), axis=1))
-        for j in range(CHUNK // 128):
-            row = k * (CHUNK // 128) + j
-            part[2 * rank + row : 2 * rank + row + 1, :] = sums[:1, j * 128 : (j + 1) * 128]
         h_sum += jnp.dot(v_proj[:, here], x16, preferred_element_type=jnp.float32)
         d_sum += jnp.dot(
             u_proj[:, here], scaled.astype(jnp.bfloat16), preferred_element_type=jnp.float32
         )
     part[:rank] = h_sum
-    part[rank : 2 * rank] = d_sum
+    part[rank:] = d_sum
     part16[:rank] = h_sum.astype(jnp.bfloat16)
     part16[rank:] = d_sum.astype(jnp.bfloat16)
     for copy in sent:
@@ -166,7 +148,7 @@
 
 def ranks_kernel(part, other, ranks, message, total):
     rows = other.shape[0]
-    value = part[:rows] + other[...].astype(jnp.float32)
+    value = part[...] + other[...].astype(jnp.float32)
     ranks[...] = value.astype(jnp.bfloat16)
     total[...] = value
     step = rows // 2 // 128
@@ -175,30 +157,28 @@
             to = i * rows // 2 + j * 128
             rank_rows = total[pl.ds(i * rows // 2 + j, 128, stride=step), :]
             message[to : to + 128, :] = rank_rows.astype(jnp.bfloat16)
-    store3(message, rows, part[rows:])
 
 
 def join_kernel(*rest):
     *blocks, message = rest
-    rows = (message.shape[0] - 128) // len(blocks)
-    bias = jnp.zeros((32, 128), jnp.float32)
+    rows = blocks[0].shape[0]
     for k, block in enumerate(blocks):
-        message[k * rows : (k + 1) * rows, :] = block[:rows, :]
-        bias += join3(block[rows:, :])
-    store3(message, len(blocks) * rows, bias)
+        message[k * rows : (k + 1) * rows, :] = block[...]
 
 
 def join_blocks(blocks):
     rows, lanes = blocks[0].shape
-    shape = jax.ShapeDtypeStruct(((rows - 128) * len(blocks) + 128, lanes), blocks[0].dtype)
+    shape = jax.ShapeDtypeStruct((rows * len(blocks), lanes), blocks[0].dtype)
     return local_call(join_kernel, shape, *blocks, mib=6)
 
 
-def grads_kernel(place, x_group, up_group, near_ranks, far_ranks, pieces, result, spread, bias_rows):
+def grads_kernel(place, x_group, up_group, near_ranks, far_ranks, pieces, result, spread):
     count, wide, lanes = x_group.shape
     ny = count // 2
     y, c = place[0], place[1]
-    both = near_ranks.shape[0] // ny // 128 * 128
+    both = near_ranks.shape[0] // ny
+    ones = jnp.ones((8, 3 * lanes), jnp.bfloat16)
+    sums = jnp.zeros((8, wide), jnp.float32)
     rank = both // 2
     for part in range(2):
         acc = jnp.zeros((rank, wide), jnp.float32)
@@ -209,10 +189,10 @@
             right = [x_group[pair + c], x_group[pair + 1 - c]]
             if part == 0:
                 ups = [up_group[pair + c], up_group[pair + 1 - c]]
-                right = [
-                    (up.astype(jnp.float32) * x.astype(jnp.float32)).astype(jnp.bfloat16)
-                    for up, x in zip(ups, right)
-                ]
+                scaled = [up.astype(jnp.float32) * x.astype(jnp.float32) for up, x in zip(ups, right)]
+                for value in scaled:
+                    sums = sums + dot_last(ones, jnp.concatenate(split3(value), axis=1))
+                right = [value.astype(jnp.bfloat16) for value in scaled]
             acc = acc + dot_last(left, jnp.concatenate(right, axis=1))
         result[:, part * wide : (part + 1) * wide] = acc
     dests, height, _ = pieces.shape
@@ -222,12 +202,9 @@
             spread[pl.ds(j * blocks + k, dests, stride=height), :] = result[
                 j * dests : (j + 1) * dests, k * lanes : (k + 1) * lanes
             ]
-    bias = join3(near_ranks[ny * both :, :]) + join3(far_ranks[ny * both :, :])
-    bias_rows[...] = bias
-    mine = (y * 2 + c) * (wide // lanes)
     first = rank // dests * blocks
     for k in range(wide // lanes):
-        row = bias_rows[pl.ds(mine + k, 1), :]
+        row = sums[:1, k * lanes : (k + 1) * lanes]
         high = row.astype(jnp.bfloat16).astype(jnp.float32)
         for i, value in enumerate((high, row - high)):
             at = first + i * (wide // lanes) + k
@@ -302,7 +279,7 @@
         forward_kernel,
         [
             array((half_width, samples), bf16),
-            array((2 * rank + half_width // 128, samples), jnp.float32),
+            array((2 * rank, samples), jnp.float32),
             array((2 * rank, samples), bf16),
         ],
         arrived,
@@ -329,7 +306,7 @@
     )
     ranks, message = local_call(
         ranks_kernel,
-        [array((2 * rank, samples), bf16), array((2 * rank + 128, samples), bf16)],
+        [array((2 * rank, samples), bf16)] * 2,
         part,
         other,
         scratch_shapes=[pltpu.VMEM((2 * rank, samples), jnp.float32)],
@@ -359,7 +336,6 @@
         scratch_shapes=[
             pltpu.VMEM((rank, 2 * wide), jnp.float32),
             pltpu.VMEM((dp_count * height, 128), jnp.float32),
-            pltpu.VMEM((32, 128), jnp.float32),
         ],
         mib=16,
     )

time: 196 us -> 196 us (level)
    ppermute x3, waiting for transfers between devices: 5.61 us -> 3.41 us  [shift(): lax.ppermute(value, axis, [(i, (i + by) % size) for i in range(size)])]
where the time goes in v5:
time: 196 us; the launch traced here: 193 us
  waiting for transfers between devices  65.2 us (33%)
  blocking collectives  58.2 us (30%)
  starting transfers between devices  30 us (15%)
  Pallas kernels  22.7 us (12%)
  matrix products  6.09 us (3%)
  other arithmetic  5.2 us (3%)
  local copies, waits for them, and re-layouts  4.53 us (2%)
    all_to_all x1, blocking collectives, step(): got = lax.all_to_all(outgoing, DP, split_axis=0, concat_axis=0, tiled=True)  58.2 us
    all_to_all x1, waiting for transfers between devices, step(): lax.all_to_all(looked, DP, split_axis=1, concat_axis=0, tiled=True)  29.2 us
    ppermute x1, waiting for transfers between devices, step(): partner = lax.ppermute(arrived, 't', SWAP)  19.6 us
    pallas_call x5, Pallas kernels, local_call(): pl.pallas_call(body, out_shape=out_shape, in_specs=specs or [SMEM] * scal...  17.4 us
    all_to_all x1, starting transfers between devices, step(): lax.all_to_all(looked, DP, split_axis=1, concat_axis=0, tiled=True)  14 us
    all_to_all x1, waiting for transfers between devices, step(): lax.all_to_all(x_zero.reshape(group, wide, samples), ('y', 'c'), split_ax...  8.63 us
    dot_general x2, matrix products, dot_first(): lax.dot_general(left, right, (((0,), (0,)), ((), ())), preferred_element_...  5.29 us
    pallas_call x1, Pallas kernels, gather(): pl.pallas_call(gather_kernel, out_shape=jax.ShapeDtypeStruct((dests, coun...  5.27 us
  transfers between devices with their start and end apart: 10, of which 6 were waited for; matrix products, arithmetic and copies ran while one was open for 6% of the time, Pallas kernels for 4%

profile of v5, /device:TPU:4, one launch (start us, length us, event | category | flops | bytes accessed | tf_op | source)
XLA Modules:
  0.0 192.7 jit_solution(12685564519631694286)
XLA Ops:
  0.7 1.2 copy-done
  1.9 1.1 copy_bitcast_fusion
  3.0 14.0 %all-to-all-start = ((bf16[32,128,128]{2,0,1:T(8,128)(2,1)}), bf16[32,128,128]{2,0,1:T(8,128)(2,1)S(1)}, u32[]{:S(2)}, u32[]{:S(2)}) async-start(bf16[32,128,128]{2,0,1:T(8,128)(2,1)} %copy_bitcast_fusion), calls=%async_computation | async-start | bytes 2097152 | tf_op jit(solution)/shard_map/all_to_all | solution.py:269
  17.1 29.2 %all-to-all-done = bf16[32,128,128]{2,0,1:T(8,128)(2,1)S(1)} async-done(((bf16[32,128,128]{2,0,1:T(8,128)(2,1)}), bf16[32,128,128]{2,0,1:T(8,128)(2,1)S(1)}, u32[]{:S(2)}, u32[]{:S(2)}) %all-to-all-start) | async-done | bytes 1048608 | tf_op jit(solution)/shard_map/all_to_all | solution.py:269
  47.1 3.8 %fusion.10 = (bf16[8192,128]{1,0:T(8,128)(2,1)S(1)}, bf16[8192,128]{1,0:T(8,128)(2,1)S(1)}) fusion(s32[8192]{0:T(1024)S(1)} %get-tuple-element.23, bf16[8192]{0:T(1024)(128)(2,1)S(1)} %get-tuple-element.26, bf16[8192]{0:T(1024)(128)(2,1)S(1)} %fusion.25), kind=kLoop, calls=%fused_computation.13 | loop fusion | flops 3145728 | bytes 4259840 | tf_op jit(solution)/shard_map/jit(_where)/select_n | solution.py:247
  52.3 19.6 %collective-permute-done.rest_1_ = bf16[4096,128]{1,0:T(8,128)(2,1)S(1)} collective-permute-done((bf16[4096,128]{1,0:T(8,128)(2,1)S(1)}, bf16[4096,128]{1,0:T(8,128)(2,1)S(1)}, u32[]{:S(2)}, u32[]{:S(2)}) %collective-permute-start) | collective-permute-done | bytes 1048608 | tf_op jit(solution)/shard_map/ppermute | solution.py:270
  72.0 1.0 copy-done.2
  72.9 8.5 %shard_map.93 = (bf16[4096,128]{1,0:T(8,128)(2,1)}, f32[768,128]{1,0:T(8,128)S(1)}, bf16[768,128]{1,0:T(8,128)(2,1)}) custom-call(bf16[4096,128]{1,0:T(8,128)(2,1)S(1)} %bitcast.30, s32[4096]{0:T(1024)} %fusion.36.rest_0_, bf16[4096,128]{1,0:T(8,128)(2,1)} %copy-done.2, bf16[4096,128]{1,0:T(8,128)(2,1)} %rest_2_.1, ...), custom_call_target="tpu_custom_call", output_to_operand_aliasing={{0}: (2, {})} | custom-call | tf_op jit(solution)/shard_map/pallas_call | solution.py:47
  82.3 3.8 %all-to-all-start.2 = ((bf16[8,512,128]{2,1,0:T(8,128)(2,1)}), bf16[8,512,128]{2,1,0:T(8,128)(2,1)S(1)}, u32[]{:S(2)}, u32[]{:S(2)}) async-start(bf16[8,512,128]{2,1,0:T(8,128)(2,1)} %bitcast.31), calls=%async_computation.2 | async-start | bytes 2097152 | tf_op jit(solution)/shard_map/all_to_all | solution.py:271
  86.1 2.8 %collective-permute-done.1.other = bf16[768,128]{1,0:T(8,128)(2,1)S(1)} collective-permute-done((bf16[768,128]{1,0:T(8,128)(2,1)}, bf16[768,128]{1,0:T(8,128)(2,1)S(1)}, u32[]{:S(2)}, u32[]{:S(2)}) %collective-permute-start.1) | collective-permute-done | bytes 196640 | tf_op jit(solution)/shard_map/ppermute | solution.py:303
  89.7 3.8 %fusion.3 = f32[4096,128]{1,0:T(8,128)S(1)} fusion(bf16[384,4096]{1,0:T(8,128)(2,1)} %rest_4_.1, bf16[4096,128]{1,0:T(8,128)(2,1)} %rest_2_.1, f32[4096]{0:T(1024)S(1)} %copy-done.4, bf16[768,128]{1,0:T(8,128)(2,1)S(1)} %get-tuple-element.15), kind=kOutput, calls=%fused_computation.5 | convolution fusion | flops 404750336 | bytes 6406144 | tf_op jit(solution)/shard_map/dot_general | solution.py:29
  93.5 1.5 fusion.4.near
  95.9 1.1 collective-permute-start.3
  97.0 3.2 %collective-permute-start.4 = (bf16[768,128]{1,0:T(8,128)(2,1)}, bf16[768,128]{1,0:T(8,128)(2,1)S(1)}, u32[]{:S(2)}, u32[]{:S(2)}) collective-permute-start(bf16[768,128]{1,0:T(8,128)(2,1)} %get-tuple-element.17.rest_0_), channel_id=1, source_target_pairs={{0,8},{4,12},{8,0},{12,4},{1,9},{5,13},{9,1},{13,5},{2,10},{6,14},... | collective-permute-start | bytes 589832 | tf_op jit(solution)/shard_map/ppermute | solution.py:35
  100.2 1.0 collective-permute-start.5
  101.2 1.5 all-to-all-done.2.up_group
  102.7 4.4 %all-to-all-start.1 = ((bf16[8,512,128]{2,1,0:T(8,128)(2,1)}), bf16[8,512,128]{2,1,0:T(8,128)(2,1)}, u32[]{:S(2)}, u32[]{:S(2)}) async-start(bf16[8,512,128]{2,1,0:T(8,128)(2,1)} %bitcast.32), calls=%async_computation.1 | async-start | bytes 2097152 | tf_op jit(solution)/shard_map/all_to_all | solution.py:304
  107.1 3.4 %collective-permute-done.4.rest_2_ = bf16[768,128]{1,0:T(8,128)(2,1)S(1)} collective-permute-done((bf16[768,128]{1,0:T(8,128)(2,1)}, bf16[768,128]{1,0:T(8,128)(2,1)S(1)}, u32[]{:S(2)}, u32[]{:S(2)}) %collective-permute-start.4) | collective-permute-done | bytes 196640 | tf_op jit(solution)/shard_map/ppermute | solution.py:35
  110.5 2.0 %shard_map.95.near_ranks = bf16[3072,128]{1,0:T(8,128)(2,1)} custom-call(bf16[768,128]{1,0:T(8,128)(2,1)} %get-tuple-element.17.rest_0_, bf16[768,128]{1,0:T(8,128)(2,1)S(1)} %collective-permute-done.3.rest_1_, bf16[768,128]{1,0:T(8,128)(2,1)S(1)} %collective-permute-done.4.rest_2_, bf16[768,128]{1,0:T(8,128)(2,1)} %collective-permute-done.5.rest_3_), custom_call_target="tpu_custom_call" | custom-call | tf_op jit(solution)/shard_map/pallas_call | solution.py:47
  114.4 8.6 %all-to-all-done.1.x_group = bf16[8,512,128]{2,1,0:T(8,128)(2,1)} async-done(((bf16[8,512,128]{2,1,0:T(8,128)(2,1)}), bf16[8,512,128]{2,1,0:T(8,128)(2,1)}, u32[]{:S(2)}, u32[]{:S(2)}) %all-to-all-start.1) | async-done | bytes 1048608 | tf_op jit(solution)/shard_map/all_to_all | solution.py:304
  123.0 4.9 %shard_map.96.extra = bf16[128,32,128]{2,1,0:T(8,128)(2,1)S(1)} custom-call(s32[2]{0:T(128)S(1)} %pad_add_fusion.place, bf16[8,512,128]{2,1,0:T(8,128)(2,1)} %all-to-all-done.1.x_group, bf16[8,512,128]{2,1,0:T(8,128)(2,1)S(1)} %all-to-all-done.2.up_group, bf16[3072,128]{1,0:T(8,128)(2,1)} %shard_map.95.near_ranks, ...), custom_call_target="tpu_custom_call" | custom-call | tf_op jit(solution)/shard_map/pallas_call | solution.py:47
  128.0 5.3 %gather_rows.1 = bf16[128,64,128]{2,1,0:T(8,128)(2,1)S(1)} custom-call(s32[4096]{0:T(1024)} %fusion.30.rows_in, bf16[4096,128]{1,0:T(8,128)(2,1)S(1)} %fusion.4.near, bf16[4096,128]{1,0:T(8,128)(2,1)} %collective-permute-done.2.far_in, bf16[128,32,128]{2,1,0:T(8,128)(2,1)S(1)} %shard_map.96.extra), custom_call_target="tpu_custom_call" | custom-call | tf_op jit(solution)/shard_map/gather_rows/pallas_call | solution.py:85
  133.2 58.2 %all_to_all.34.refs_0_ = bf16[128,64,128]{2,1,0:T(8,128)(2,1)S(1)} all-to-all(bf16[128,64,128]{2,1,0:T(8,128)(2,1)S(1)} %gather_rows.1), channel_id=1, replica_groups=mesh['z'=8,'xl'=2,'y'=4,'c'=2,'t'=2] {'z','xl','y','c'}, dimensions={0} | all-to-all | bytes 4194304 | tf_op jit(solution)/shard_map/all_to_all | solution.py:348
  191.4 1.3 shard_map.97
  (26 shorter events, 6.8 us)
Async XLA Ops:
  0.6 1.2 copy-start
  0.6 16.4 %copy-start.3 = (s32[8192]{0:T(1024)S(1)}, s32[8192]{0:T(1024)}, u32[]{:S(2)}) copy-start(s32[8192]{0:T(1024)} %param.7) | copy-start | bytes 98308
  3.0 43.2 %all-to-all-start = ((bf16[32,128,128]{2,0,1:T(8,128)(2,1)}), bf16[32,128,128]{2,0,1:T(8,128)(2,1)S(1)}, u32[]{:S(2)}, u32[]{:S(2)}) async-start(bf16[32,128,128]{2,0,1:T(8,128)(2,1)} %copy_bitcast_fusion), calls=%async_computation | async-start | bytes 2097152 | tf_op jit(solution)/shard_map/all_to_all | solution.py:269
  46.3 25.7 %collective-permute-start = (bf16[4096,128]{1,0:T(8,128)(2,1)S(1)}, bf16[4096,128]{1,0:T(8,128)(2,1)S(1)}, u32[]{:S(2)}, u32[]{:S(2)}) collective-permute-start(bf16[4096,128]{1,0:T(8,128)(2,1)S(1)} %bitcast.29), channel_id=1, source_target_pairs={{0,1},{1,0},{2,3},{3,2},{4,5},{5,4},{6,7},{7,6},{8,9},{9,8},{10,11... | collective-permute-start | bytes 3145736 | tf_op jit(solution)/shard_map/ppermute | solution.py:270
  72.0 1.0 copy-start.2
  81.4 8.2 %copy-start.4 = (f32[4096]{0:T(1024)S(1)}, f32[4096]{0:T(1024)}, u32[]{:S(2)}) copy-start(f32[4096]{0:T(1024)} %param.10) | copy-start | bytes 49156
  81.5 7.5 %collective-permute-start.1 = (bf16[768,128]{1,0:T(8,128)(2,1)}, bf16[768,128]{1,0:T(8,128)(2,1)S(1)}, u32[]{:S(2)}, u32[]{:S(2)}) collective-permute-start(bf16[768,128]{1,0:T(8,128)(2,1)} %get-tuple-element.14), channel_id=1, source_target_pairs={{0,1},{1,0},{2,3},{3,2},{4,5},{5,4},{6,7},{7,6},{8,9},{9,8},{10,11... | collective-permute-start | bytes 589832 | tf_op jit(solution)/shard_map/ppermute | solution.py:303
  82.3 20.3 %all-to-all-start.2 = ((bf16[8,512,128]{2,1,0:T(8,128)(2,1)}), bf16[8,512,128]{2,1,0:T(8,128)(2,1)S(1)}, u32[]{:S(2)}, u32[]{:S(2)}) async-start(bf16[8,512,128]{2,1,0:T(8,128)(2,1)} %bitcast.31), calls=%async_computation.2 | async-start | bytes 2097152 | tf_op jit(solution)/shard_map/all_to_all | solution.py:271
  89.7 3.8 %copy-start.1 = (bf16[384,4096]{1,0:T(8,128)(2,1)S(1)}, bf16[384,4096]{1,0:T(8,128)(2,1)}, u32[]{:S(2)}) copy-start(bf16[384,4096]{1,0:T(8,128)(2,1)} %rest_3_.1) | copy-start | bytes 9437188
  95.0 32.9 %collective-permute-start.2 = (bf16[4096,128]{1,0:T(8,128)(2,1)S(1)}, bf16[4096,128]{1,0:T(8,128)(2,1)}, u32[]{:S(2)}, u32[]{:S(2)}) collective-permute-start(bf16[4096,128]{1,0:T(8,128)(2,1)S(1)} %fusion.4.near), channel_id=1, source_target_pairs={{0,1},{1,0},{2,3},{3,2},{4,5},{5,4},{6,7},{7,6},{8,9},{9,8},{10,11... | collective-permute-start | bytes 3145736 | tf_op jit(solution)/shard_map/ppermute | solution.py:319
  95.9 11.2 %collective-permute-start.3 = (bf16[768,128]{1,0:T(8,128)(2,1)}, bf16[768,128]{1,0:T(8,128)(2,1)S(1)}, u32[]{:S(2)}, u32[]{:S(2)}) collective-permute-start(bf16[768,128]{1,0:T(8,128)(2,1)} %get-tuple-element.17.rest_0_), channel_id=1, source_target_pairs={{0,4},{4,8},{8,12},{12,0},{1,5},{5,9},{9,13},{13,1},{2,6},{6,10},{... | collective-permute-start | bytes 589832 | tf_op jit(solution)/shard_map/ppermute | solution.py:35
  97.0 13.5 %collective-permute-start.4 = (bf16[768,128]{1,0:T(8,128)(2,1)}, bf16[768,128]{1,0:T(8,128)(2,1)S(1)}, u32[]{:S(2)}, u32[]{:S(2)}) collective-permute-start(bf16[768,128]{1,0:T(8,128)(2,1)} %get-tuple-element.17.rest_0_), channel_id=1, source_target_pairs={{0,8},{4,12},{8,0},{12,4},{1,9},{5,13},{9,1},{13,5},{2,10},{6,14},... | collective-permute-start | bytes 589832 | tf_op jit(solution)/shard_map/ppermute | solution.py:35
  100.2 10.3 %collective-permute-start.5 = (bf16[768,128]{1,0:T(8,128)(2,1)}, bf16[768,128]{1,0:T(8,128)(2,1)}, u32[]{:S(2)}, u32[]{:S(2)}) collective-permute-start(bf16[768,128]{1,0:T(8,128)(2,1)} %get-tuple-element.17.rest_0_), channel_id=1, source_target_pairs={{0,12},{4,0},{8,4},{12,8},{1,13},{5,1},{9,5},{13,9},{2,14},{6,2},{... | collective-permute-start | bytes 589832 | tf_op jit(solution)/shard_map/ppermute | solution.py:35
  102.7 20.4 %all-to-all-start.1 = ((bf16[8,512,128]{2,1,0:T(8,128)(2,1)}), bf16[8,512,128]{2,1,0:T(8,128)(2,1)}, u32[]{:S(2)}, u32[]{:S(2)}) async-start(bf16[8,512,128]{2,1,0:T(8,128)(2,1)} %bitcast.32), calls=%async_computation.1 | async-start | bytes 2097152 | tf_op jit(solution)/shard_map/all_to_all | solution.py:304
  112.5 10.6 %collective-permute-start.6 = (bf16[3072,128]{1,0:T(8,128)(2,1)}, bf16[3072,128]{1,0:T(8,128)(2,1)}, u32[]{:S(2)}, u32[]{:S(2)}) collective-permute-start(bf16[3072,128]{1,0:T(8,128)(2,1)} %shard_map.95.near_ranks), channel_id=1, source_target_pairs={{0,2},{2,0},{1,3},{3,1},{4,6},{6,4},{5,7},{7,5},{8,10},{10,8},{9,1... | collective-permute-start | bytes 2359304 | tf_op jit(solution)/shard_map/ppermute | solution.py:325

commit v6 on v5

--- a/solution.py
+++ b/solution.py
@@ -10,7 +10,7 @@
 
 DP = ("z", "xl", "y", "c")
 SWAP = [(0, 1), (1, 0)]
-UNROLL = 32
+UNROLL = 64
 CHUNK = 512
 
 
@@ -122,6 +122,11 @@
     table[half:] = far[...].astype(jnp.float32)
     copies[0].wait()
     pick_rows(rows, table, picked)
+    for k in range(half // CHUNK):
+        here = slice(k * CHUNK, (k + 1) * CHUNK)
+        staged[here, :] = picked[here, :].astype(jnp.bfloat16)
+        sent.append(pltpu.make_async_copy(staged.at[here], x_out.at[here], sems.at[5 + k]))
+        sent[-1].start()
     for copy in copies[2:]:
         copy.wait()
     h_sum = jnp.zeros((rank, lanes), jnp.float32)
@@ -131,9 +136,6 @@
         x = picked[here, :]
         scaled = upstream[here, :].astype(jnp.float32) * x
         x16 = x.astype(jnp.bfloat16)
-        staged[here, :] = x16
-        sent.append(pltpu.make_async_copy(staged.at[here], x_out.at[here], sems.at[5 + k]))
-        sent[-1].start()
         h_sum += jnp.dot(v_proj[:, here], x16, preferred_element_type=jnp.float32)
         d_sum += jnp.dot(
             u_proj[:, here], scaled.astype(jnp.bfloat16), preferred_element_type=jnp.float32

time: 196 us -> 195 us (level)
  transfers between devices with their start and end apart: 10 -> 10, of which waited for: 6 -> 6; matrix products, arithmetic and copies ran while one was open for 6% -> 7% of each run, Pallas kernels for 4% -> 4%
where the time goes in v6:
time: 195 us; the launch traced here: 192 us
  waiting for transfers between devices  65.2 us (33%)
  blocking collectives  58.2 us (30%)
  starting transfers between devices  30 us (15%)
  Pallas kernels  21.5 us (11%)
  matrix products  6.09 us (3%)
  other arithmetic  5.2 us (3%)
  local copies, waits for them, and re-layouts  4.53 us (2%)
    all_to_all x1, blocking collectives, step(): got = lax.all_to_all(outgoing, DP, split_axis=0, concat_axis=0, tiled=True)  58.2 us
    all_to_all x1, waiting for transfers between devices, step(): lax.all_to_all(looked, DP, split_axis=1, concat_axis=0, tiled=True)  29.2 us
    ppermute x1, waiting for transfers between devices, step(): partner = lax.ppermute(arrived, 't', SWAP)  19.6 us
    pallas_call x5, Pallas kernels, local_call(): pl.pallas_call(body, out_shape=out_shape, in_specs=specs or [SMEM] * scal...  16.5 us
    all_to_all x1, starting transfers between devices, step(): lax.all_to_all(looked, DP, split_axis=1, concat_axis=0, tiled=True)  14 us
    all_to_all x1, waiting for transfers between devices, step(): lax.all_to_all(x_zero.reshape(group, wide, samples), ('y', 'c'), split_ax...  8.63 us
    dot_general x2, matrix products, dot_first(): lax.dot_general(left, right, (((0,), (0,)), ((), ())), preferred_element_...  5.29 us
    ppermute x3, starting transfers between devices, shift(): lax.ppermute(value, axis, [(i, (i + by) % size) for i in range(size)])  5.28 us
  transfers between devices with their start and end apart: 10, of which 6 were waited for; matrix products, arithmetic and copies ran while one was open for 7% of the time, Pallas kernels for 4%

profile of v6, /device:TPU:4, one launch (start us, length us, event | category | flops | bytes accessed | tf_op | source)
XLA Modules:
  0.0 191.5 jit_solution(14351659156727344948)
XLA Ops:
  0.7 1.2 copy-done
  1.9 1.1 copy_bitcast_fusion
  3.0 14.0 %all-to-all-start = ((bf16[32,128,128]{2,0,1:T(8,128)(2,1)}), bf16[32,128,128]{2,0,1:T(8,128)(2,1)S(1)}, u32[]{:S(2)}, u32[]{:S(2)}) async-start(bf16[32,128,128]{2,0,1:T(8,128)(2,1)} %copy_bitcast_fusion), calls=%async_computation | async-start | bytes 2097152 | tf_op jit(solution)/shard_map/all_to_all | solution.py:271
  17.1 29.2 %all-to-all-done = bf16[32,128,128]{2,0,1:T(8,128)(2,1)S(1)} async-done(((bf16[32,128,128]{2,0,1:T(8,128)(2,1)}), bf16[32,128,128]{2,0,1:T(8,128)(2,1)S(1)}, u32[]{:S(2)}, u32[]{:S(2)}) %all-to-all-start) | async-done | bytes 1048608 | tf_op jit(solution)/shard_map/all_to_all | solution.py:271
  47.1 3.8 %fusion.10 = (bf16[8192,128]{1,0:T(8,128)(2,1)S(1)}, bf16[8192,128]{1,0:T(8,128)(2,1)S(1)}) fusion(s32[8192]{0:T(1024)S(1)} %get-tuple-element.23, bf16[8192]{0:T(1024)(128)(2,1)S(1)} %get-tuple-element.26, bf16[8192]{0:T(1024)(128)(2,1)S(1)} %fusion.25), kind=kLoop, calls=%fused_computation.13 | loop fusion | flops 3145728 | bytes 4259840 | tf_op jit(solution)/shard_map/jit(_where)/select_n | solution.py:249
  52.3 19.6 %collective-permute-done.rest_1_ = bf16[4096,128]{1,0:T(8,128)(2,1)S(1)} collective-permute-done((bf16[4096,128]{1,0:T(8,128)(2,1)S(1)}, bf16[4096,128]{1,0:T(8,128)(2,1)S(1)}, u32[]{:S(2)}, u32[]{:S(2)}) %collective-permute-start) | collective-permute-done | bytes 1048608 | tf_op jit(solution)/shard_map/ppermute | solution.py:272
  72.0 1.0 copy-done.2
  72.9 7.6 %shard_map.93 = (bf16[4096,128]{1,0:T(8,128)(2,1)}, f32[768,128]{1,0:T(8,128)S(1)}, bf16[768,128]{1,0:T(8,128)(2,1)}) custom-call(bf16[4096,128]{1,0:T(8,128)(2,1)S(1)} %bitcast.30, s32[4096]{0:T(1024)} %fusion.36.rest_0_, bf16[4096,128]{1,0:T(8,128)(2,1)} %copy-done.2, bf16[4096,128]{1,0:T(8,128)(2,1)} %rest_2_.1, ...), custom_call_target="tpu_custom_call", output_to_operand_aliasing={{0}: (2, {})} | custom-call | tf_op jit(solution)/shard_map/pallas_call | solution.py:47
  81.4 3.8 %all-to-all-start.2 = ((bf16[8,512,128]{2,1,0:T(8,128)(2,1)}), bf16[8,512,128]{2,1,0:T(8,128)(2,1)S(1)}, u32[]{:S(2)}, u32[]{:S(2)}) async-start(bf16[8,512,128]{2,1,0:T(8,128)(2,1)} %bitcast.31), calls=%async_computation.2 | async-start | bytes 2097152 | tf_op jit(solution)/shard_map/all_to_all | solution.py:273
  85.2 2.8 %collective-permute-done.1.other = bf16[768,128]{1,0:T(8,128)(2,1)S(1)} collective-permute-done((bf16[768,128]{1,0:T(8,128)(2,1)}, bf16[768,128]{1,0:T(8,128)(2,1)S(1)}, u32[]{:S(2)}, u32[]{:S(2)}) %collective-permute-start.1) | collective-permute-done | bytes 196640 | tf_op jit(solution)/shard_map/ppermute | solution.py:305
  88.8 3.8 %fusion.3 = f32[4096,128]{1,0:T(8,128)S(1)} fusion(bf16[384,4096]{1,0:T(8,128)(2,1)} %rest_4_.1, bf16[4096,128]{1,0:T(8,128)(2,1)} %rest_2_.1, f32[4096]{0:T(1024)S(1)} %copy-done.4, bf16[768,128]{1,0:T(8,128)(2,1)S(1)} %get-tuple-element.15), kind=kOutput, calls=%fused_computation.5 | convolution fusion | flops 404750336 | bytes 6406144 | tf_op jit(solution)/shard_map/dot_general | solution.py:29
  92.6 1.5 fusion.4.near
  95.0 1.1 collective-permute-start.3
  96.1 3.2 %collective-permute-start.4 = (bf16[768,128]{1,0:T(8,128)(2,1)}, bf16[768,128]{1,0:T(8,128)(2,1)S(1)}, u32[]{:S(2)}, u32[]{:S(2)}) collective-permute-start(bf16[768,128]{1,0:T(8,128)(2,1)} %get-tuple-element.17.rest_0_), channel_id=1, source_target_pairs={{0,8},{4,12},{8,0},{12,4},{1,9},{5,13},{9,1},{13,5},{2,10},{6,14},... | collective-permute-start | bytes 589832 | tf_op jit(solution)/shard_map/ppermute | solution.py:35
  99.3 1.0 collective-permute-start.5
  100.3 1.5 all-to-all-done.2.up_group
  101.8 4.4 %all-to-all-start.1 = ((bf16[8,512,128]{2,1,0:T(8,128)(2,1)}), bf16[8,512,128]{2,1,0:T(8,128)(2,1)}, u32[]{:S(2)}, u32[]{:S(2)}) async-start(bf16[8,512,128]{2,1,0:T(8,128)(2,1)} %bitcast.32), calls=%async_computation.1 | async-start | bytes 2097152 | tf_op jit(solution)/shard_map/all_to_all | solution.py:306
  106.2 3.4 %collective-permute-done.4.rest_2_ = bf16[768,128]{1,0:T(8,128)(2,1)S(1)} collective-permute-done((bf16[768,128]{1,0:T(8,128)(2,1)}, bf16[768,128]{1,0:T(8,128)(2,1)S(1)}, u32[]{:S(2)}, u32[]{:S(2)}) %collective-permute-start.4) | collective-permute-done | bytes 196640 | tf_op jit(solution)/shard_map/ppermute | solution.py:35
  109.6 2.0 %shard_map.95.near_ranks = bf16[3072,128]{1,0:T(8,128)(2,1)} custom-call(bf16[768,128]{1,0:T(8,128)(2,1)} %get-tuple-element.17.rest_0_, bf16[768,128]{1,0:T(8,128)(2,1)S(1)} %collective-permute-done.3.rest_1_, bf16[768,128]{1,0:T(8,128)(2,1)S(1)} %collective-permute-done.4.rest_2_, bf16[768,128]{1,0:T(8,128)(2,1)} %collective-permute-done.5.rest_3_), custom_call_target="tpu_custom_call" | custom-call | tf_op jit(solution)/shard_map/pallas_call | solution.py:47
  113.5 8.6 %all-to-all-done.1.x_group = bf16[8,512,128]{2,1,0:T(8,128)(2,1)} async-done(((bf16[8,512,128]{2,1,0:T(8,128)(2,1)}), bf16[8,512,128]{2,1,0:T(8,128)(2,1)}, u32[]{:S(2)}, u32[]{:S(2)}) %all-to-all-start.1) | async-done | bytes 1048608 | tf_op jit(solution)/shard_map/all_to_all | solution.py:306
  122.1 4.9 %shard_map.96.extra = bf16[128,32,128]{2,1,0:T(8,128)(2,1)S(1)} custom-call(s32[2]{0:T(128)S(1)} %pad_add_fusion.place, bf16[8,512,128]{2,1,0:T(8,128)(2,1)} %all-to-all-done.1.x_group, bf16[8,512,128]{2,1,0:T(8,128)(2,1)S(1)} %all-to-all-done.2.up_group, bf16[3072,128]{1,0:T(8,128)(2,1)} %shard_map.95.near_ranks, ...), custom_call_target="tpu_custom_call" | custom-call | tf_op jit(solution)/shard_map/pallas_call | solution.py:47
  127.1 5.0 %gather_rows.1 = bf16[128,64,128]{2,1,0:T(8,128)(2,1)S(1)} custom-call(s32[4096]{0:T(1024)} %fusion.30.rows_in, bf16[4096,128]{1,0:T(8,128)(2,1)S(1)} %fusion.4.near, bf16[4096,128]{1,0:T(8,128)(2,1)} %collective-permute-done.2.far_in, bf16[128,32,128]{2,1,0:T(8,128)(2,1)S(1)} %shard_map.96.extra), custom_call_target="tpu_custom_call" | custom-call | tf_op jit(solution)/shard_map/gather_rows/pallas_call | solution.py:85
  132.1 58.2 %all_to_all.34.refs_0_ = bf16[128,64,128]{2,1,0:T(8,128)(2,1)S(1)} all-to-all(bf16[128,64,128]{2,1,0:T(8,128)(2,1)S(1)} %gather_rows.1), channel_id=1, replica_groups=mesh['z'=8,'xl'=2,'y'=4,'c'=2,'t'=2] {'z','xl','y','c'}, dimensions={0} | all-to-all | bytes 4194304 | tf_op jit(solution)/shard_map/all_to_all | solution.py:350
  190.2 1.3 shard_map.97
  (26 shorter events, 6.7 us)
Async XLA Ops:
  0.6 1.2 copy-start
  0.6 16.4 %copy-start.3 = (s32[8192]{0:T(1024)S(1)}, s32[8192]{0:T(1024)}, u32[]{:S(2)}) copy-start(s32[8192]{0:T(1024)} %param.7) | copy-start | bytes 98308
  3.0 43.2 %all-to-all-start = ((bf16[32,128,128]{2,0,1:T(8,128)(2,1)}), bf16[32,128,128]{2,0,1:T(8,128)(2,1)S(1)}, u32[]{:S(2)}, u32[]{:S(2)}) async-start(bf16[32,128,128]{2,0,1:T(8,128)(2,1)} %copy_bitcast_fusion), calls=%async_computation | async-start | bytes 2097152 | tf_op jit(solution)/shard_map/all_to_all | solution.py:271
  46.3 25.7 %collective-permute-start = (bf16[4096,128]{1,0:T(8,128)(2,1)S(1)}, bf16[4096,128]{1,0:T(8,128)(2,1)S(1)}, u32[]{:S(2)}, u32[]{:S(2)}) collective-permute-start(bf16[4096,128]{1,0:T(8,128)(2,1)S(1)} %bitcast.29), channel_id=1, source_target_pairs={{0,1},{1,0},{2,3},{3,2},{4,5},{5,4},{6,7},{7,6},{8,9},{9,8},{10,11... | collective-permute-start | bytes 3145736 | tf_op jit(solution)/shard_map/ppermute | solution.py:272
  72.0 1.0 copy-start.2
  80.5 8.2 %copy-start.4 = (f32[4096]{0:T(1024)S(1)}, f32[4096]{0:T(1024)}, u32[]{:S(2)}) copy-start(f32[4096]{0:T(1024)} %param.10) | copy-start | bytes 49156
  80.5 7.5 %collective-permute-start.1 = (bf16[768,128]{1,0:T(8,128)(2,1)}, bf16[768,128]{1,0:T(8,128)(2,1)S(1)}, u32[]{:S(2)}, u32[]{:S(2)}) collective-permute-start(bf16[768,128]{1,0:T(8,128)(2,1)} %get-tuple-element.14), channel_id=1, source_target_pairs={{0,1},{1,0},{2,3},{3,2},{4,5},{5,4},{6,7},{7,6},{8,9},{9,8},{10,11... | collective-permute-start | bytes 589832 | tf_op jit(solution)/shard_map/ppermute | solution.py:305
  81.4 20.3 %all-to-all-start.2 = ((bf16[8,512,128]{2,1,0:T(8,128)(2,1)}), bf16[8,512,128]{2,1,0:T(8,128)(2,1)S(1)}, u32[]{:S(2)}, u32[]{:S(2)}) async-start(bf16[8,512,128]{2,1,0:T(8,128)(2,1)} %bitcast.31), calls=%async_computation.2 | async-start | bytes 2097152 | tf_op jit(solution)/shard_map/all_to_all | solution.py:273
  88.8 3.8 %copy-start.1 = (bf16[384,4096]{1,0:T(8,128)(2,1)S(1)}, bf16[384,4096]{1,0:T(8,128)(2,1)}, u32[]{:S(2)}) copy-start(bf16[384,4096]{1,0:T(8,128)(2,1)} %rest_3_.1) | copy-start | bytes 9437188
  94.1 33.0 %collective-permute-start.2 = (bf16[4096,128]{1,0:T(8,128)(2,1)S(1)}, bf16[4096,128]{1,0:T(8,128)(2,1)}, u32[]{:S(2)}, u32[]{:S(2)}) collective-permute-start(bf16[4096,128]{1,0:T(8,128)(2,1)S(1)} %fusion.4.near), channel_id=1, source_target_pairs={{0,1},{1,0},{2,3},{3,2},{4,5},{5,4},{6,7},{7,6},{8,9},{9,8},{10,11... | collective-permute-start | bytes 3145736 | tf_op jit(solution)/shard_map/ppermute | solution.py:321
  95.0 11.2 %collective-permute-start.3 = (bf16[768,128]{1,0:T(8,128)(2,1)}, bf16[768,128]{1,0:T(8,128)(2,1)S(1)}, u32[]{:S(2)}, u32[]{:S(2)}) collective-permute-start(bf16[768,128]{1,0:T(8,128)(2,1)} %get-tuple-element.17.rest_0_), channel_id=1, source_target_pairs={{0,4},{4,8},{8,12},{12,0},{1,5},{5,9},{9,13},{13,1},{2,6},{6,10},{... | collective-permute-start | bytes 589832 | tf_op jit(solution)/shard_map/ppermute | solution.py:35
  96.1 13.5 %collective-permute-start.4 = (bf16[768,128]{1,0:T(8,128)(2,1)}, bf16[768,128]{1,0:T(8,128)(2,1)S(1)}, u32[]{:S(2)}, u32[]{:S(2)}) collective-permute-start(bf16[768,128]{1,0:T(8,128)(2,1)} %get-tuple-element.17.rest_0_), channel_id=1, source_target_pairs={{0,8},{4,12},{8,0},{12,4},{1,9},{5,13},{9,1},{13,5},{2,10},{6,14},... | collective-permute-start | bytes 589832 | tf_op jit(solution)/shard_map/ppermute | solution.py:35
  99.3 10.3 %collective-permute-start.5 = (bf16[768,128]{1,0:T(8,128)(2,1)}, bf16[768,128]{1,0:T(8,128)(2,1)}, u32[]{:S(2)}, u32[]{:S(2)}) collective-permute-start(bf16[768,128]{1,0:T(8,128)(2,1)} %get-tuple-element.17.rest_0_), channel_id=1, source_target_pairs={{0,12},{4,0},{8,4},{12,8},{1,13},{5,1},{9,5},{13,9},{2,14},{6,2},{... | collective-permute-start | bytes 589832 | tf_op jit(solution)/shard_map/ppermute | solution.py:35
  101.8 20.4 %all-to-all-start.1 = ((bf16[8,512,128]{2,1,0:T(8,128)(2,1)}), bf16[8,512,128]{2,1,0:T(8,128)(2,1)}, u32[]{:S(2)}, u32[]{:S(2)}) async-start(bf16[8,512,128]{2,1,0:T(8,128)(2,1)} %bitcast.32), calls=%async_computation.1 | async-start | bytes 2097152 | tf_op jit(solution)/shard_map/all_to_all | solution.py:306
  111.6 10.6 %collective-permute-start.6 = (bf16[3072,128]{1,0:T(8,128)(2,1)}, bf16[3072,128]{1,0:T(8,128)(2,1)}, u32[]{:S(2)}, u32[]{:S(2)}) collective-permute-start(bf16[3072,128]{1,0:T(8,128)(2,1)} %shard_map.95.near_ranks), channel_id=1, source_target_pairs={{0,2},{2,0},{1,3},{3,1},{4,6},{6,4},{5,7},{7,5},{8,10},{10,8},{9,1... | collective-permute-start | bytes 2359304 | tf_op jit(solution)/shard_map/ppermute | solution.py:327
